TPU v7x, 256 devices: a whole 4x4x8 slice. The times are simulated.
256 devices in a mesh: seq: 16 (over z, core), kvh: 8 (over y_hi, x), batch: 2 (over y_lo).
Axes of the slice: x: 4, y: 4 (y_hi: 2, y_lo: 2; y = y_hi * 2 + y_lo), z: 8, core: 2. Of those that a mesh axis runs over, the one named last changes fastest.
Arguments:
- query: bfloat16 [4096, 5120], P(('batch', 'seq'), 'kvh'), parts along dimension 0, may hold values from -33.3 to 33.3
- self_keys: bfloat16 [4096, 1024], P(('batch', 'seq'), 'kvh'), parts along dimension 0, may hold values from -6.4 to 6.4
- self_values: bfloat16 [4096, 1024], P(('batch', 'seq'), 'kvh'), parts along dimension 0, may hold values from -6 to 6
- cache_keys: bfloat16 [16384, 1024], P(('batch', 'seq'), 'kvh'), parts along dimension 0, may hold values from -6.375 to 6.375
- cache_values: bfloat16 [16384, 1024], P(('batch', 'seq'), 'kvh'), parts along dimension 0, may hold values from -6 to 6
- cache_pos: int32 [16384], P(('batch', 'seq')), parts along dimension 0, may hold values from 0 to 8191, each once
- d_out: bfloat16 [4096, 5120], P(('batch', 'seq'), 'kvh'), parts along dimension 0, may hold values from -6 to 6
Outputs:
- attended: bfloat16 [4096, 5120], P(('batch', 'seq'), 'kvh'), parts along dimension 0
- grad_query: bfloat16 [4096, 5120], P(('batch', 'seq'), 'kvh'), parts along dimension 0
- grad_keys: bfloat16 [4096, 1024], P(('batch', 'seq'), 'kvh'), parts along dimension 0
- grad_values: bfloat16 [4096, 1024], P(('batch', 'seq'), 'kvh'), parts along dimension 0
There are 2 independent parts, one for each index of `batch`. A program takes and returns all parts, laid end to end along the dimension named above; each array names one. Nothing has to cross between parts.
Inputs may be any that keep to these rules, and one draw needn't show every extreme that they name: `cache_pos`: each cache position appears once.
All inputs are finite; a program needn't handle non-finite values.
Results may differ from a plain program's by a relative error of at most 0.012.
The roundings to bfloat16 on the way count: a program that leaves them out, or rounds other values in their place, can miss the bound.
Values may be sent and summed in bfloat16 or wider, within the bound.
No kernel may reach another device: no remote copies, remote signals or barrier semaphores. Data moves between devices by JAX's collectives and lax.ppermute only.
A program may use at most 64 MiB of HBM per device.

v0:
```python
import functools

import jax
import jax.numpy as jnp
from jax import lax
from jax.experimental import pallas as pl
from jax.experimental.pallas import tpu as pltpu
from jax.sharding import PartitionSpec as P


HD = 128
GROUP = 5
WINDOW = 512
LANES = 128
BLOCK = 32
NEG = -1e30
SCALE = HD**-0.5
EXP2_SCALE = SCALE * 1.4426950408889634
POS_BASE = 128
POS_ROWS = 16


def nt(a, b):
    return lax.dot_general(a, b, (((1,), (1,)), ((), ())), preferred_element_type=jnp.float32)


def nn(a, b):
    return lax.dot_general(a, b, (((1,), (0,)), ((), ())), preferred_element_type=jnp.float32)


def tn(a, b):
    return lax.dot_general(a, b, (((0,), (0,)), ((), ())), preferred_element_type=jnp.float32)


def cuts(width, step):
    return [slice(i, i + step) for i in range(0, width, step)]


def positions_of(digits, groups):
    wide = digits.astype(jnp.float32)
    return wide[:groups] * POS_BASE + wide[groups : 2 * groups]


def row_bound(base, rows, start_pos):
    row = lax.broadcasted_iota(jnp.int32, (rows, LANES), 0)
    bound = start_pos + jnp.maximum(base + row - (WINDOW - 1), 0)
    return bound.astype(jnp.float32)


def window_visible(base, rows, window, g):
    row = lax.broadcasted_iota(jnp.int32, (rows, LANES), 0)
    key = lax.broadcasted_iota(jnp.int32, (rows, LANES), 1) + g * LANES
    first = window - rows
    return (key <= row + first) & (key >= row + (first - WINDOW + 1)) & (key >= first - base)


def accumulate(parts, row_max, row_sum, rs):
    old = row_max[rs, :]
    best = old
    for part in parts:
        best = jnp.maximum(best, part)
    added = row_sum[rs, :] * jnp.exp2((old - best) * EXP2_SCALE)
    raised = [jnp.exp2((part - best) * EXP2_SCALE) for part in parts]
    for part in raised:
        added = added + part
    row_max[rs, :] = best
    row_sum[rs, :] = added
    return raised, best


def packet_stats(queries, keys, digits, bound, state, rows, t):
    row_max, row_sum, raised_ref, level_ref = state
    lanes = cuts(keys.shape[0], LANES)
    positions = positions_of(digits, len(lanes))
    scores = nt(queries, keys)
    for rs in cuts(rows * GROUP, BLOCK):
        inner = slice(rs.start % rows, rs.start % rows + BLOCK)
        limit = bound[inner]
        parts = [
            jnp.where(positions[g : g + 1] < limit, scores[rs, ls], NEG)
            for g, ls in enumerate(lanes)
        ]
        raised, best = accumulate(parts, row_max, row_sum, rs)
        for ls, part in zip(lanes, raised):
            raised_ref[t, rs, ls] = part
        level_ref[t, rs, :] = best


def stats_kernel(*refs, rows, tile, start_pos, counts, done, with_window):
    meta_ref = refs[0]
    first_packet = 2 if done else 3
    packets = refs[first_packet : first_packet + len(counts)]
    at = first_packet + len(counts) + (5 if with_window else 0) + (4 if done else 0)
    outs = refs[at:]
    state = outs[:4]
    if done:
        queries_ref = refs[1]
    else:
        queries_ref, grads_ref = outs[4:]
        for h in range(GROUP):
            queries_ref[h * rows : (h + 1) * rows, :] = refs[1][:, h * HD : (h + 1) * HD]
            grads_ref[h * rows : (h + 1) * rows, :] = refs[2][:, h * HD : (h + 1) * HD]
    row_max, row_sum = state[:2]
    base = meta_ref[0] * rows
    bound = row_bound(base, rows, start_pos)
    if done:
        max_in, sum_in = refs[at - 4 : at - 2]
        row_max[...] = max_in[...]
        row_sum[...] = sum_in[...]
    else:
        row_max[...] = jnp.full(row_max.shape, NEG, jnp.float32)
        row_sum[...] = jnp.zeros(row_sum.shape, jnp.float32)
    t = done
    for packet, count in zip(packets, counts):

        def one(n, carry, packet=packet, t=t):
            packet_stats(
                queries_ref[...],
                packet[n, :tile, :],
                packet[n, tile : tile + POS_ROWS, :],
                bound,
                state,
                rows,
                t + n,
            )
            return carry

        lax.fori_loop(0, count, one, 0)
        t += count
    if with_window:
        self_raised, self_level, window_ref = outs[4:]
        own, up_one, swapped_one, up_two, swapped_two = refs[first_packet + len(counts) :][:5]
        even = meta_ref[0] % 2 == 0

        def place(blocks):
            for d, block in enumerate(blocks):
                window_ref[d * rows : (d + 1) * rows, :] = block

        @pl.when(even)
        def _():
            place([up_two[0], up_two[1], up_one[0], up_one[1], own[0]])

        @pl.when(jnp.logical_not(even))
        def _():
            place([swapped_two[1], swapped_one[0], swapped_one[1], own[1], own[0]])

        window = window_ref.shape[0]
        scores = nt(queries_ref[...], window_ref[:, :HD])
        lanes = cuts(window, LANES)
        shown = [window_visible(base, rows, window, g) for g in range(len(lanes))]
        for rs in cuts(rows * GROUP, BLOCK):
            inner = slice(rs.start % rows, rs.start % rows + BLOCK)
            parts = [
                jnp.where(shown[g][inner], scores[rs, ls], NEG) for g, ls in enumerate(lanes)
            ]
            raised, best = accumulate(parts, row_max, row_sum, rs)
            for ls, part in zip(lanes, raised):
                self_raised[rs, ls] = part
            self_level[rs, :] = best


WHOLE = pl.BlockSpec(memory_space=pltpu.VMEM)
ANYWHERE = pl.BlockSpec(memory_space=pl.ANY)
SCALARS = pl.BlockSpec(memory_space=pltpu.SMEM)
LIMIT = pltpu.CompilerParams(vmem_limit_bytes=6 * 1024 * 1024)


def f32(*shape):
    return jax.ShapeDtypeStruct(shape, jnp.float32)


def bf16(*shape):
    return jax.ShapeDtypeStruct(shape, jnp.bfloat16)


def stats(my_index, inputs, previous, packets, selfs, done, tiles, rows, tile, start_pos):
    total = rows * GROUP
    counts = tuple(p.shape[0] for p in packets)
    operands = [my_index, *inputs, *packets]
    outs = [f32(total, LANES), f32(total, LANES), f32(tiles, total, tile), f32(tiles, total, LANES)]
    aliases = {}
    if selfs is not None:
        operands += list(selfs)
        span = (WINDOW // rows + 1) * rows
        outs += [f32(total, span), f32(total, LANES), bf16(span, 2 * HD)]
    if previous is None:
        outs += [bf16(total, HD)] * 2
    else:
        aliases = {len(operands) + 2: 2, len(operands) + 3: 3}
        operands += list(previous)
    keys = sum(counts) * tile
    return pl.pallas_call(
        functools.partial(
            stats_kernel,
            rows=rows,
            tile=tile,
            start_pos=start_pos,
            counts=counts,
            done=done,
            with_window=selfs is not None,
        ),
        in_specs=[SCALARS] + [WHOLE] * (len(operands) - 1),
        out_specs=[WHOLE] * len(outs),
        out_shape=outs,
        input_output_aliases=aliases,
        compiler_params=LIMIT,
        cost_estimate=pl.CostEstimate(
            flops=2 * total * HD * keys, transcendentals=total * keys, bytes_accessed=2 * keys * HD
        ),
        name="stats",
    )(*operands)


def fetch_all(packets, counts, held, sems, width):
    copies = []
    at = 0
    for n, count in enumerate(counts):
        copy = pltpu.make_async_copy(
            packets[n].at[:, pl.ds(0, width), :], held.at[pl.ds(at, count)], sems.at[n]
        )
        copy.start()
        copies.append(copy)
        at += count
    return copies


def value_kernel(*refs, rows, tile, counts):
    n = len(counts)
    (queries, grads, window_ref, max_in, sum_in, raised, level, self_raised, self_level) = refs[:9]
    key_packets = refs[9 : 9 + n]
    value_packets = refs[9 + n : 9 + 2 * n]
    outs = refs[9 + 2 * n :]
    (attended_ref, factor_ref, delta, partial_ref, keys, values, own_ref) = outs[:7]
    rim = window_ref.shape[0] // rows - 1
    back_refs = outs[7 : 7 + rim]
    (top_ref, inverse_ref, summed, self_weights, key_sems, value_sems) = outs[7 + rim :]
    copies = fetch_all(value_packets, counts, values, value_sems, tile)
    key_copies = fetch_all(key_packets, counts, keys, key_sems, tile)
    total = rows * GROUP
    window = window_ref.shape[0]
    tiles = sum(counts)
    heads = cuts(total, rows)
    cols = cuts(GROUP * HD, HD)
    lanes = cuts(tile, LANES)
    self_lanes = cuts(window, LANES)
    first = window - rows
    for hs in heads:
        best = max_in[hs, :]
        top = jnp.max(best, axis=1, keepdims=True)
        scaled = sum_in[hs, :] * jnp.exp2((best - top) * EXP2_SCALE)
        top_ref[hs, :] = jnp.broadcast_to(top, (rows, LANES))
        inverse = 1.0 / jnp.sum(scaled, axis=1, keepdims=True)
        inverse_ref[hs, :] = jnp.broadcast_to(inverse, (rows, LANES))

    parts = []
    for hs in heads:
        factor = jnp.exp2((self_level[hs, :] - top_ref[hs, :]) * EXP2_SCALE) * inverse_ref[hs, :]
        pieces = []
        for ls in self_lanes:
            weight = self_raised[hs, ls] * factor
            self_weights[hs, ls] = weight
            pieces.append(weight.astype(jnp.bfloat16))
        parts.append(jnp.concatenate(pieces, axis=1))
    rounded = jnp.concatenate(parts, axis=0)
    summed[...] = nn(rounded, window_ref[:, HD:])
    value_grads = tn(rounded, grads[...])
    own_ref[:, HD:] = value_grads[first:, :]
    for d, back_ref in enumerate(back_refs):
        back_ref[:, HD:] = value_grads[d * rows : (d + 1) * rows, :].astype(jnp.bfloat16)
    for copy in copies:
        copy.wait()

    def value_pass(t, carry):
        parts = []
        for hs in heads:
            factor = jnp.exp2((level[t, hs, :] - top_ref[hs, :]) * EXP2_SCALE) * inverse_ref[hs, :]
            factor_ref[t, hs, :] = factor
            pieces = [(raised[t, hs, ls] * factor).astype(jnp.bfloat16) for ls in lanes]
            parts.append(jnp.concatenate(pieces, axis=1))
        summed[...] += nn(jnp.concatenate(parts, axis=0), values[t])
        return carry

    lax.fori_loop(0, tiles, value_pass, 0)
    for hs, cs in zip(heads, cols):
        out = summed[hs, :].astype(jnp.bfloat16)
        attended_ref[:, cs] = out
        products = out.astype(jnp.float32) * grads[hs, :].astype(jnp.float32)
        delta[hs, :] = jnp.broadcast_to(jnp.sum(products, axis=1, keepdims=True), (rows, LANES))

    grad_weights = nt(grads[...], window_ref[:, HD:])
    parts = []
    for hs in heads:
        shift = delta[hs, :]
        pieces = [
            (self_weights[hs, ls] * (grad_weights[hs, ls] - shift)).astype(jnp.bfloat16)
            for ls in self_lanes
        ]
        parts.append(jnp.concatenate(pieces, axis=1))
    grad_scores = jnp.concatenate(parts, axis=0)
    partial_ref[...] = nn(grad_scores, window_ref[:, :HD])
    key_grads = tn(grad_scores, queries[...])
    own_ref[:, :HD] = key_grads[first:, :]
    for d, back_ref in enumerate(back_refs):
        back_ref[:, :HD] = key_grads[d * rows : (d + 1) * rows, :].astype(jnp.bfloat16)
    for copy in key_copies:
        copy.wait()


def grad_kernel(
    grads, raised, factor_ref, delta, partial_ref, keys, values, out_ref, *scratch, rows, span, last
):
    heads = cuts(rows * GROUP, rows)
    cols = cuts(GROUP * HD, HD)
    lanes = cuts(keys.shape[1], LANES)
    summed = scratch[0] if last else out_ref
    summed[...] = partial_ref[...]

    def grad_pass(t, carry):
        grad_weights = nt(grads[...], values[t])
        parts = []
        for hs in heads:
            shift = delta[hs, :]
            factor = factor_ref[t, hs, :]
            pieces = [
                (raised[t, hs, ls] * factor * (grad_weights[hs, ls] - shift)).astype(jnp.bfloat16)
                for ls in lanes
            ]
            parts.append(jnp.concatenate(pieces, axis=1))
        summed[...] += nn(jnp.concatenate(parts, axis=0), keys[t])
        return carry

    lax.fori_loop(*span, grad_pass, 0)
    if last:
        for hs, cs in zip(heads, cols):
            out_ref[:, cs] = (summed[hs, :] * SCALE).astype(jnp.bfloat16)


def combine_kernel(own_ref, *refs):
    total = own_ref[...]
    for ref in refs[:-2]:
        total = total + ref[...].astype(jnp.float32)
    refs[-2][...] = (total[:, :HD] * SCALE).astype(jnp.bfloat16)
    refs[-1][...] = total[:, HD:].astype(jnp.bfloat16)


def value_stage(queries, grads, window, state, key_packets, value_packets, rows, tile):
    counts = tuple(p.shape[0] for p in value_packets)
    tiles = sum(counts)
    total = rows * GROUP
    span = window.shape[0]
    rim = span // rows - 1
    return pl.pallas_call(
        functools.partial(value_kernel, rows=rows, tile=tile, counts=counts),
        in_specs=[WHOLE] * 9 + [ANYWHERE] * (2 * len(counts)),
        out_specs=[WHOLE] * (7 + rim),
        out_shape=[
            bf16(rows, GROUP * HD),
            f32(tiles, total, LANES),
            f32(total, LANES),
            f32(total, HD),
            bf16(tiles, tile, HD),
            bf16(tiles, tile, HD),
            f32(rows, 2 * HD),
        ]
        + [bf16(rows, 2 * HD)] * rim,
        scratch_shapes=[
            pltpu.VMEM((total, LANES), jnp.float32),
            pltpu.VMEM((total, LANES), jnp.float32),
            pltpu.VMEM((total, HD), jnp.float32),
            pltpu.VMEM((total, span), jnp.float32),
            pltpu.SemaphoreType.DMA((len(counts),)),
            pltpu.SemaphoreType.DMA((len(counts),)),
        ],
        input_output_aliases={6: 1},
        compiler_params=LIMIT,
        cost_estimate=pl.CostEstimate(
            flops=2 * total * HD * tiles * tile, transcendentals=0, bytes_accessed=tiles * tile * HD
        ),
        name="value_stage",
    )(queries, grads, window, *state, *key_packets, *value_packets)


def grad_stage(grads, raised, factor, delta, partial, keys, values, rows, span, last):
    tiles, tile, _ = keys.shape
    total = rows * GROUP
    return pl.pallas_call(
        functools.partial(grad_kernel, rows=rows, span=span, last=last),
        in_specs=[WHOLE] * 7,
        out_specs=WHOLE,
        out_shape=bf16(rows, GROUP * HD) if last else f32(total, HD),
        scratch_shapes=[pltpu.VMEM((total, HD), jnp.float32)] if last else [],
        compiler_params=LIMIT,
        cost_estimate=pl.CostEstimate(
            flops=4 * total * HD * (span[1] - span[0]) * tile,
            transcendentals=0,
            bytes_accessed=tiles * tile * HD,
        ),
        name="grad_stage",
    )(grads, raised, factor, delta, partial, keys, values)


def combine(own, returned):
    rows = own.shape[0]
    return pl.pallas_call(
        combine_kernel,
        in_specs=[WHOLE] * (1 + len(returned)),
        out_specs=[WHOLE] * 2,
        out_shape=[bf16(rows, HD)] * 2,
        compiler_params=LIMIT,
        name="combine",
    )(own, *returned)


def compute(index, query, d_out, key_groups, value_groups, selfs, selfs_at, shape):
    rows, tile, start_pos = shape
    tiles = sum(p.shape[0] for group in key_groups for p in group)
    state, done = None, 0
    for n, group in enumerate(key_groups):
        inputs = [queries] if done else [query, d_out]
        extra = selfs if n == selfs_at else None
        outs = stats(index, inputs, state, group, extra, done, tiles, rows, tile, start_pos)
        state = outs[:4]
        if not done:
            queries, grads = outs[4:]
        elif extra is not None:
            *self_state, window = outs[4:]
        done += sum(p.shape[0] for p in group)
    key_packets = [p for group in key_groups for p in group]
    value_packets = [p for group in value_groups for p in group]
    attended, factor, delta, partial, keys, values, own, *back = value_stage(
        queries, grads, window, [*state, *self_state], key_packets, value_packets, rows, tile
    )

    def finish():
        shared = (grads, state[2], factor, delta)
        summed = grad_stage(*shared, partial, keys, values, rows, (0, tiles // 2), False)
        return grad_stage(*shared, summed, keys, values, rows, (tiles // 2, tiles), True)

    return attended, finish, own, back


def local(query, self_keys, self_values, cache_keys, cache_values, cache_pos, d_out):
    rows = query.shape[0]
    tile = cache_keys.shape[0]
    peers = lax.axis_size("seq")
    my_index = lax.axis_index("seq")
    start_pos = (tile - rows) * peers
    rim = (WINDOW + rows - 2) // rows
    chips = peers // 2

    partner = [(i, i ^ 1) for i in range(peers)]
    ring = [(2 * z, 2 * ((z + 1) % chips)) for z in range(chips)]
    ring += [(2 * z + 1, 2 * ((z - 1) % chips) + 1) for z in range(chips)]

    def swap(block):
        return lax.ppermute(block, "seq", partner)

    def turn(block):
        return lax.ppermute(block, "seq", ring)

    digits = jnp.concatenate([cache_pos // POS_BASE, cache_pos % POS_BASE]).astype(jnp.bfloat16)
    digits = digits.reshape(2 * tile // HD, HD)
    digits = jnp.pad(digits, ((0, POS_ROWS - digits.shape[0]), (0, 0)))
    own_keys = jnp.concatenate([cache_keys, digits])[None]
    own_values = cache_values[None]
    own_self = jnp.concatenate([self_keys, self_values], axis=1)[None]
    key_block = jnp.concatenate([own_keys, swap(own_keys)])
    value_block = jnp.concatenate([own_values, swap(own_values)])
    other_self = swap(own_self)
    self_block = jnp.concatenate([own_self, other_self])
    key_groups, value_groups, selfs = [(key_block,)], [(value_block,)], [self_block]
    for step in range(1, chips // 2 + 1):
        key_block = turn(key_block)
        value_block = turn(value_block)
        if step == chips // 2:
            key_groups.append((key_block,))
            value_groups.append((value_block,))
        else:
            key_groups.append((key_block, swap(key_block)))
            value_groups.append((value_block, swap(value_block)))
        if step <= 2:
            self_block = turn(self_block)
            selfs += [self_block, swap(self_block)]

    index = my_index.reshape(1)
    attended, finish, own, back = compute(
        index, query, d_out, key_groups, value_groups, selfs, 3, (rows, tile, start_pos)
    )
    returned = []
    for distance in range(1, rim + 1):
        route = [(i, i - distance) for i in range(distance, peers)]
        returned.append(lax.ppermute(back[rim - distance], "seq", route))
    grad_query = finish()
    grad_keys, grad_values = combine(own, returned)
    return attended, grad_query, grad_keys, grad_values


def solution(mesh):
    split = P(("batch", "seq"), "kvh")
    return jax.shard_map(
        local,
        mesh=mesh,
        in_specs=(split,) * 5 + (P(("batch", "seq")), split),
        out_specs=(split,) * 4,
        check_vma=False,
    )
```

profile of v0, /device:TPU:194, one launch (start us, length us, event | category | flops | bytes accessed | tf_op | source)
XLA Modules:
  0.0 86.9 jit_solution(10283378758365267118)
XLA Ops:
  0.6 0.7 fusion.7
  1.3 0.9 %maximum_bitcast_fusion = bf16[1,528,128]{2,1,0:T(8,128)(2,1)S(1)} fusion(bf16[16,128]{1,0:T(8,128)(2,1)S(1)} %fusion.2, bf16[512,128]{1,0:T(8,128)(2,1)} %param.10), kind=kLoop, calls=%fused_computation.2 | loop fusion | flops 270336 | bytes 270336 | tf_op jit(solution)/shard_map/broadcast_in_dim | solution.py:464
  2.4 1.3 %collective-permute-done = bf16[1,528,128]{2,1,0:T(8,128)(2,1)S(1)} collective-permute-done((bf16[1,528,128]{2,1,0:T(8,128)(2,1)S(1)}, bf16[1,528,128]{2,1,0:T(8,128)(2,1)S(1)}, u32[]{:S(2)}, u32[]{:S(2)}) %collective-permute-start) | collective-permute-done | bytes 135200 | tf_op jit(solution)/shard_map/ppermute | solution.py:456
  3.7 1.1 %collective-permute-start.1 = (bf16[2,528,128]{2,1,0:T(8,128)(2,1)S(1)}, bf16[2,528,128]{2,1,0:T(8,128)(2,1)S(1)}, u32[]{:S(2)}, u32[]{:S(2)}) collective-permute-start(bf16[2,528,128]{2,1,0:T(8,128)(2,1)S(1)} %pad_maximum_fusion.refs_3_.refs_9_), channel_id=1, source_target_pairs={{0,32},{32,64},{64,96},{96,128},{128,160},{160,192},{192,224},{224... | collective-permute-start | bytes 811016 | tf_op jit(solution)/shard_map/ppermute | solution.py:459
  4.8 5.4 %collective-permute-done.1.refs_2_.refs_10_ = bf16[2,528,128]{2,1,0:T(8,128)(2,1)S(1)} collective-permute-done((bf16[2,528,128]{2,1,0:T(8,128)(2,1)S(1)}, bf16[2,528,128]{2,1,0:T(8,128)(2,1)S(1)}, u32[]{:S(2)}, u32[]{:S(2)}) %collective-permute-start.1) | collective-permute-done | bytes 270368 | tf_op jit(solution)/shard_map/ppermute | solution.py:459
  10.3 1.0 %collective-permute-start.2 = (bf16[2,528,128]{2,1,0:T(8,128)(2,1)S(1)}, bf16[2,528,128]{2,1,0:T(8,128)(2,1)S(1)}, u32[]{:S(2)}, u32[]{:S(2)}) collective-permute-start(bf16[2,528,128]{2,1,0:T(8,128)(2,1)S(1)} %collective-permute-done.1.refs_2_.refs_10_), channel_id=1, source_target_pairs={{0,32},{32,64},{64,96},{96,128},{128,160},{160,192},{192,224},{224... | collective-permute-start | bytes 811016 | tf_op jit(solution)/shard_map/ppermute | solution.py:459
  11.3 0.9 %pad_maximum_fusion.1.refs_17_ = bf16[2,512,128]{2,1,0:T(8,128)(2,1)S(1)} fusion(bf16[1,512,128]{2,1,0:T(8,128)(2,1)S(1)} %collective-permute-done.13, bf16[1,512,128]{2,1,0:T(8,128)(2,1)} %bitcast.11), kind=kLoop, calls=%fused_computation.1 | loop fusion | flops 131072 | bytes 524288 | tf_op jit(solution)/shard_map/concatenate | solution.py:468
  12.2 1.3 %collective-permute-start.14 = (bf16[2,512,128]{2,1,0:T(8,128)(2,1)S(1)}, bf16[2,512,128]{2,1,0:T(8,128)(2,1)}, u32[]{:S(2)}, u32[]{:S(2)}) collective-permute-start(bf16[2,512,128]{2,1,0:T(8,128)(2,1)S(1)} %pad_maximum_fusion.1.refs_17_), channel_id=1, source_target_pairs={{0,32},{32,64},{64,96},{96,128},{128,160},{160,192},{192,224},{224... | collective-permute-start | bytes 786440 | tf_op jit(solution)/shard_map/ppermute | solution.py:459
  13.5 0.8 maximum_bitcast_fusion.1
  14.4 2.3 %collective-permute-done.2.refs_2_.refs_12_ = bf16[2,528,128]{2,1,0:T(8,128)(2,1)S(1)} collective-permute-done((bf16[2,528,128]{2,1,0:T(8,128)(2,1)S(1)}, bf16[2,528,128]{2,1,0:T(8,128)(2,1)S(1)}, u32[]{:S(2)}, u32[]{:S(2)}) %collective-permute-start.2) | collective-permute-done | bytes 270368 | tf_op jit(solution)/shard_map/ppermute | solution.py:459
  16.7 1.0 %collective-permute-start.3 = (bf16[2,528,128]{2,1,0:T(8,128)(2,1)S(1)}, bf16[2,528,128]{2,1,0:T(8,128)(2,1)}, u32[]{:S(2)}, u32[]{:S(2)}) collective-permute-start(bf16[2,528,128]{2,1,0:T(8,128)(2,1)S(1)} %collective-permute-done.2.refs_2_.refs_12_), channel_id=1, source_target_pairs={{0,32},{32,64},{64,96},{96,128},{128,160},{160,192},{192,224},{224... | collective-permute-start | bytes 811016 | tf_op jit(solution)/shard_map/ppermute | solution.py:459
  17.8 2.5 %collective-permute-start.6 = (bf16[2,128,256]{2,1,0:T(8,128)(2,1)S(1)}, bf16[2,128,256]{2,1,0:T(8,128)(2,1)S(1)}, u32[]{:S(2)}, u32[]{:S(2)}) collective-permute-start(bf16[2,128,256]{2,1,0:T(8,128)(2,1)S(1)} %pad_maximum_fusion.2.refs_4_), channel_id=1, source_target_pairs={{0,32},{32,64},{64,96},{96,128},{128,160},{160,192},{192,224},{224... | collective-permute-start | bytes 393224 | tf_op jit(solution)/shard_map/ppermute | solution.py:459
  20.3 0.4 collective-permute-start.16
  20.7 3.9 %collective-permute-done.6.refs_5_ = bf16[2,128,256]{2,1,0:T(8,128)(2,1)S(1)} collective-permute-done((bf16[2,128,256]{2,1,0:T(8,128)(2,1)S(1)}, bf16[2,128,256]{2,1,0:T(8,128)(2,1)S(1)}, u32[]{:S(2)}, u32[]{:S(2)}) %collective-permute-start.6) | collective-permute-done | bytes 131104 | tf_op jit(solution)/shard_map/ppermute | solution.py:459
  24.6 1.3 %collective-permute-start.8 = (bf16[2,128,256]{2,1,0:T(8,128)(2,1)S(1)}, bf16[2,128,256]{2,1,0:T(8,128)(2,1)S(1)}, u32[]{:S(2)}, u32[]{:S(2)}) collective-permute-start(bf16[2,128,256]{2,1,0:T(8,128)(2,1)S(1)} %collective-permute-done.6.refs_5_), channel_id=1, source_target_pairs={{0,32},{32,64},{64,96},{96,128},{128,160},{160,192},{192,224},{224... | collective-permute-start | bytes 393224 | tf_op jit(solution)/shard_map/ppermute | solution.py:459
  25.9 0.7 copy-done.10
  26.6 1.3 %collective-permute-start.11 = (bf16[2,528,128]{2,1,0:T(8,128)(2,1)S(1)}, bf16[2,528,128]{2,1,0:T(8,128)(2,1)S(1)}, u32[]{:S(2)}, u32[]{:S(2)}) collective-permute-start(bf16[2,528,128]{2,1,0:T(8,128)(2,1)S(1)} %collective-permute-done.1.refs_2_.refs_10_), channel_id=1, source_target_pairs={{0,16},{16,0},{32,48},{48,32},{64,80},{80,64},{96,112},{112,96},{1... | collective-permute-start | bytes 811016 | tf_op jit(solution)/shard_map/ppermute | solution.py:456
  27.9 0.7 copy-done.12
  28.6 0.7 copy-done
  29.3 0.5 collective-permute-start.4
  29.8 2.1 %collective-permute-start.18 = (bf16[2,512,128]{2,1,0:T(8,128)(2,1)}, bf16[2,512,128]{2,1,0:T(8,128)(2,1)}, u32[]{:S(2)}, u32[]{:S(2)}) collective-permute-start(bf16[2,512,128]{2,1,0:T(8,128)(2,1)} %collective-permute-done.16.refs_20_), channel_id=1, source_target_pairs={{0,32},{32,64},{64,96},{96,128},{128,160},{160,192},{192,224},{224... | collective-permute-start | bytes 786440 | tf_op jit(solution)/shard_map/ppermute | solution.py:459
  31.9 0.9 %collective-permute-start.9 = (bf16[2,128,256]{2,1,0:T(8,128)(2,1)S(1)}, bf16[2,128,256]{2,1,0:T(8,128)(2,1)S(1)}, u32[]{:S(2)}, u32[]{:S(2)}) collective-permute-start(bf16[2,128,256]{2,1,0:T(8,128)(2,1)S(1)} %collective-permute-done.8.refs_7_), channel_id=1, source_target_pairs={{0,16},{16,0},{32,48},{48,32},{64,80},{80,64},{96,112},{112,96},{1... | collective-permute-start | bytes 393224 | tf_op jit(solution)/shard_map/ppermute | solution.py:456
  32.8 0.6 copy-done.14
  33.5 0.3 collective-permute-done.9.refs_8_
  33.8 0.6 copy-done.16
  34.5 0.7 copy-done.2
  35.2 0.8 collective-permute-start.15
  36.0 1.7 %collective-permute-done.18.refs_22_ = bf16[2,512,128]{2,1,0:T(8,128)(2,1)} collective-permute-done((bf16[2,512,128]{2,1,0:T(8,128)(2,1)}, bf16[2,512,128]{2,1,0:T(8,128)(2,1)}, u32[]{:S(2)}, u32[]{:S(2)}) %collective-permute-start.18) | collective-permute-done | bytes 262176 | tf_op jit(solution)/shard_map/ppermute | solution.py:459
  37.7 0.7 copy-done.4
  38.4 0.5 collective-permute-start.19
  38.9 0.7 copy-done.6
  39.6 0.9 %collective-permute-start.20 = (bf16[2,512,128]{2,1,0:T(8,128)(2,1)}, bf16[2,512,128]{2,1,0:T(8,128)(2,1)}, u32[]{:S(2)}, u32[]{:S(2)}) collective-permute-start(bf16[2,512,128]{2,1,0:T(8,128)(2,1)} %collective-permute-done.18.refs_22_), channel_id=1, source_target_pairs={{0,32},{32,64},{64,96},{96,128},{128,160},{160,192},{192,224},{224... | collective-permute-start | bytes 786440 | tf_op jit(solution)/shard_map/ppermute | solution.py:459
  40.5 0.9 %copy-done.18 = bf16[128,640]{1,0:T(8,128)(2,1)S(1)} copy-done((bf16[128,640]{1,0:T(8,128)(2,1)S(1)}, bf16[128,640]{1,0:T(8,128)(2,1)}, u32[]{:S(2)}) %copy-start.18) | copy-done | bytes 163864
  41.4 0.9 %copy-done.19 = bf16[128,640]{1,0:T(8,128)(2,1)S(1)} copy-done((bf16[128,640]{1,0:T(8,128)(2,1)S(1)}, bf16[128,640]{1,0:T(8,128)(2,1)}, u32[]{:S(2)}) %copy-start.19) | copy-done | bytes 163864
  42.3 1.2 %stats.5 = (f32[640,128]{1,0:T(8,128)S(1)}, f32[640,128]{1,0:T(8,128)S(1)}, f32[16,640,512]{2,1,0:T(8,128)S(1)}, f32[16,640,128]{2,1,0:T(8,128)S(1)}, bf16[640,1...) custom-call(s32[1]{0:T(128)} %bitcast.refs_0_, bf16[128,640]{1,0:T(8,128)(2,1)S(1)} %copy-done.18, ...), custom_call_target="tpu_custom_call" | custom-call | flops 167772160 | bytes 262144 | tf_op jit(solution)/shard_map/stats/pallas_call | solution.py:192
  43.5 0.9 %copy-done.3 = bf16[2,528,128]{2,1,0:T(8,128)(2,1)S(1)} copy-done((bf16[2,528,128]{2,1,0:T(8,128)(2,1)S(1)}, bf16[2,528,128]{2,1,0:T(8,128)(2,1)}, u32[]{:S(2)}) %copy-start.3) | copy-done | bytes 270360
  44.5 2.2 %stats.6 = (f32[640,128]{1,0:T(8,128)S(1)}, f32[640,128]{1,0:T(8,128)S(1)}, f32[16,640,512]{2,1,0:T(8,128)S(1)}, f32[16,640,128]{2,1,0:T(8,128)S(1)}) custom-call(s32[1]{0:T(128)} %bitcast.refs_0_, bf16[640,128]{1,0:T(8,128)(2,1)S(1)} %get-tuple-element.42.refs_1_.refs_0_, ...), custom_call_target="tpu_custom_call", output_to_operand_aliasing={{2}: (6, {}), {3}: (7, {})} | custom-call | flops 335544320 | bytes 524288 | tf_op jit(solution)/shard_map/stats/pallas_call | solution.py:192
  46.7 2.2 %stats.7 = (f32[640,128]{1,0:T(8,128)S(1)}, f32[640,128]{1,0:T(8,128)S(1)}, f32[16,640,512]{2,1,0:T(8,128)S(1)}, f32[16,640,128]{2,1,0:T(8,128)S(1)}) custom-call(s32[1]{0:T(128)} %bitcast.refs_0_, bf16[640,128]{1,0:T(8,128)(2,1)S(1)} %get-tuple-element.42.refs_1_.refs_0_, ...), custom_call_target="tpu_custom_call", output_to_operand_aliasing={{2}: (6, {}), {3}: (7, {})} | custom-call | flops 335544320 | bytes 524288 | tf_op jit(solution)/shard_map/stats/pallas_call | solution.py:192
  49.0 3.8 %stats.8 = (f32[640,128]{1,0:T(8,128)S(1)}, f32[640,128]{1,0:T(8,128)S(1)}, f32[16,640,512]{2,1,0:T(8,128)S(1)}, f32[16,640,128]{2,1,0:T(8,128)S(1)}, f32[640,64...) custom-call(s32[1]{0:T(128)} %bitcast.refs_0_, ...), custom_call_target="tpu_custom_call", output_to_operand_aliasing={{2}: (11, {}), {3}: (12, {})} | custom-call | flops 335544320 | bytes 524288 | tf_op jit(solution)/shard_map/stats/pallas_call | solution.py:192
  52.9 2.1 %stats.9 = (f32[640,128]{1,0:T(8,128)S(1)}, f32[640,128]{1,0:T(8,128)S(1)}, f32[16,640,512]{2,1,0:T(8,128)S(1)}, f32[16,640,128]{2,1,0:T(8,128)S(1)}) custom-call(s32[1]{0:T(128)} %bitcast.refs_0_, bf16[640,128]{1,0:T(8,128)(2,1)S(1)} %get-tuple-element.42.refs_1_.refs_0_, ...), custom_call_target="tpu_custom_call", output_to_operand_aliasing={{2}: (5, {}), {3}: (6, {})} | custom-call | flops 167772160 | bytes 262144 | tf_op jit(solution)/shard_map/stats/pallas_call | solution.py:192
  55.0 8.7 %value_stage.1 = (bf16[128,640]{1,0:T(8,128)(2,1)}, f32[16,640,128]{2,1,0:T(8,128)S(1)}, f32[640,128]{1,0:T(8,128)S(1)}, f32[640,128]{1,0:T(8,128)S(1)}, bf16[16...) custom-call(bf16[640,128]{1,0:T(8,128)(2,1)S(1)} %get-tuple-element., ...), custom_call_target="tpu_custom_call", output_to_operand_aliasing={{1}: (6, {})} | custom-call | flops 1342177280 | bytes 1048576 | tf_op jit(solution)/shard_map/value_stage/pallas_call | solution.py:352
  63.8 4.0 %collective-permute-start.21 = (bf16[128,256]{1,0:T(8,128)(2,1)S(1)}, bf16[128,256]{1,0:T(8,128)(2,1)S(1)}, u32[]{:S(2)}, u32[]{:S(2)}) collective-permute-start(bf16[128,256]{1,0:T(8,128)(2,1)S(1)} %get-tuple-element.74), channel_id=1, source_target_pairs={{16,0},{32,16},{48,32},{64,48},{80,64},{96,80},{112,96},{128,112},... | collective-permute-start | bytes 196616 | tf_op jit(solution)/shard_map/ppermute | solution.py:492
  67.8 3.8 %collective-permute-start.22 = (bf16[128,256]{1,0:T(8,128)(2,1)S(1)}, bf16[128,256]{1,0:T(8,128)(2,1)S(1)}, u32[]{:S(2)}, u32[]{:S(2)}) collective-permute-start(bf16[128,256]{1,0:T(8,128)(2,1)S(1)} %get-tuple-element.75), channel_id=1, source_target_pairs={{32,0},{48,16},{64,32},{80,48},{96,64},{112,80},{128,96},{144,112}... | collective-permute-start | bytes 196616 | tf_op jit(solution)/shard_map/ppermute | solution.py:492
  71.6 3.2 %collective-permute-start.23 = (bf16[128,256]{1,0:T(8,128)(2,1)S(1)}, bf16[128,256]{1,0:T(8,128)(2,1)S(1)}, u32[]{:S(2)}, u32[]{:S(2)}) collective-permute-start(bf16[128,256]{1,0:T(8,128)(2,1)S(1)} %get-tuple-element.76), channel_id=1, source_target_pairs={{48,0},{64,16},{80,32},{96,48},{112,64},{128,80},{144,96},{160,112... | collective-permute-start | bytes 196616 | tf_op jit(solution)/shard_map/ppermute | solution.py:492
  74.8 2.1 %collective-permute-start.24 = (bf16[128,256]{1,0:T(8,128)(2,1)S(1)}, bf16[128,256]{1,0:T(8,128)(2,1)S(1)}, u32[]{:S(2)}, u32[]{:S(2)}) collective-permute-start(bf16[128,256]{1,0:T(8,128)(2,1)S(1)} %get-tuple-element.77), channel_id=1, source_target_pairs={{64,0},{80,16},{96,32},{112,48},{128,64},{144,80},{160,96},{176,11... | collective-permute-start | bytes 196616 | tf_op jit(solution)/shard_map/ppermute | solution.py:492
  76.9 4.3 %grad_stage.2.partial_ref = f32[640,128]{1,0:T(8,128)S(1)} custom-call(bf16[640,128]{1,0:T(8,128)(2,1)S(1)} %get-tuple-element.43.refs_1_.grads, f32[16,640,512]{2,1,0:T(8,128)S(1)} %get-tuple-element.63.refs_5_.raised, f32[16,640,128]{2,1,0:T(8,128)S(1)} %get-tuple-element.68.factor_ref, f32[640,128]{1,0:T(8,128)S(1)} %get-tuple-element.69.delta, ...), custom_call_target="tpu_custom_call" | custom-call | flops 1342177280 | bytes 1048576 | tf_op jit(solution)/shard_map/grad_stage/pallas_call | solution.py:386
  81.2 5.0 %grad_stage.3 = bf16[128,640]{1,0:T(8,128)(2,1)} custom-call(bf16[640,128]{1,0:T(8,128)(2,1)S(1)} %get-tuple-element.43.refs_1_.grads, f32[16,640,512]{2,1,0:T(8,128)S(1)} %get-tuple-element.63.refs_5_.raised, f32[16,640,128]{2,1,0:T(8,128)S(1)} %get-tuple-element.68.factor_ref, f32[640,128]{1,0:T(8,128)S(1)} %get-tuple-element.69.delta, ...), custom_call_target="tpu_custom_call" | custom-call | flops 1342177280 | bytes 1048576 | tf_op jit(solution)/shard_map/grad_stage/pallas_call | solution.py:386
  86.2 0.7 combine.1
  (58 shorter events, 0.4 us)
Async XLA Ops:
  2.3 1.4 %collective-permute-start = (bf16[1,528,128]{2,1,0:T(8,128)(2,1)S(1)}, bf16[1,528,128]{2,1,0:T(8,128)(2,1)S(1)}, u32[]{:S(2)}, u32[]{:S(2)}) collective-permute-start(bf16[1,528,128]{2,1,0:T(8,128)(2,1)S(1)} %maximum_bitcast_fusion), channel_id=1, source_target_pairs={{0,16},{16,0},{32,48},{48,32},{64,80},{80,64},{96,112},{112,96},{1... | collective-permute-start | bytes 405512 | tf_op jit(solution)/shard_map/ppermute | solution.py:456
  3.7 6.5 %collective-permute-start.1 = (bf16[2,528,128]{2,1,0:T(8,128)(2,1)S(1)}, bf16[2,528,128]{2,1,0:T(8,128)(2,1)S(1)}, u32[]{:S(2)}, u32[]{:S(2)}) collective-permute-start(bf16[2,528,128]{2,1,0:T(8,128)(2,1)S(1)} %pad_maximum_fusion.refs_3_.refs_9_), channel_id=1, source_target_pairs={{0,32},{32,64},{64,96},{96,128},{128,160},{160,192},{192,224},{224... | collective-permute-start | bytes 811016 | tf_op jit(solution)/shard_map/ppermute | solution.py:459
  4.8 6.5 %collective-permute-start.13 = (bf16[1,512,128]{2,1,0:T(8,128)(2,1)}, bf16[1,512,128]{2,1,0:T(8,128)(2,1)S(1)}, u32[]{:S(2)}, u32[]{:S(2)}) collective-permute-start(bf16[1,512,128]{2,1,0:T(8,128)(2,1)} %bitcast.10), channel_id=1, source_target_pairs={{0,16},{16,0},{32,48},{48,32},{64,80},{80,64},{96,112},{112,96},{1... | collective-permute-start | bytes 393224 | tf_op jit(solution)/shard_map/ppermute | solution.py:456
  10.3 6.5 %collective-permute-start.2 = (bf16[2,528,128]{2,1,0:T(8,128)(2,1)S(1)}, bf16[2,528,128]{2,1,0:T(8,128)(2,1)S(1)}, u32[]{:S(2)}, u32[]{:S(2)}) collective-permute-start(bf16[2,528,128]{2,1,0:T(8,128)(2,1)S(1)} %collective-permute-done.1.refs_2_.refs_10_), channel_id=1, source_target_pairs={{0,32},{32,64},{64,96},{96,128},{128,160},{160,192},{192,224},{224... | collective-permute-start | bytes 811016 | tf_op jit(solution)/shard_map/ppermute | solution.py:459
  12.2 26.7 %copy-start.8 = (bf16[2,512,128]{2,1,0:T(8,128)(2,1)}, bf16[2,512,128]{2,1,0:T(8,128)(2,1)S(1)}, u32[]{:S(2)}) copy-start(bf16[2,512,128]{2,1,0:T(8,128)(2,1)S(1)} %pad_maximum_fusion.1.refs_17_) | copy-start | bytes 786436
  12.2 8.0 %collective-permute-start.14 = (bf16[2,512,128]{2,1,0:T(8,128)(2,1)S(1)}, bf16[2,512,128]{2,1,0:T(8,128)(2,1)}, u32[]{:S(2)}, u32[]{:S(2)}) collective-permute-start(bf16[2,512,128]{2,1,0:T(8,128)(2,1)S(1)} %pad_maximum_fusion.1.refs_17_), channel_id=1, source_target_pairs={{0,32},{32,64},{64,96},{96,128},{128,160},{160,192},{192,224},{224... | collective-permute-start | bytes 786440 | tf_op jit(solution)/shard_map/ppermute | solution.py:459
  14.3 3.4 %collective-permute-start.5 = (bf16[1,128,256]{2,1,0:T(8,128)(2,1)S(1)}, bf16[1,128,256]{2,1,0:T(8,128)(2,1)S(1)}, u32[]{:S(2)}, u32[]{:S(2)}) collective-permute-start(bf16[1,128,256]{2,1,0:T(8,128)(2,1)S(1)} %maximum_bitcast_fusion.1), channel_id=1, source_target_pairs={{0,16},{16,0},{32,48},{48,32},{64,80},{80,64},{96,112},{112,96},{1... | collective-permute-start | bytes 196616 | tf_op jit(solution)/shard_map/ppermute | solution.py:456
  16.7 12.5 %collective-permute-start.3 = (bf16[2,528,128]{2,1,0:T(8,128)(2,1)S(1)}, bf16[2,528,128]{2,1,0:T(8,128)(2,1)}, u32[]{:S(2)}, u32[]{:S(2)}) collective-permute-start(bf16[2,528,128]{2,1,0:T(8,128)(2,1)S(1)} %collective-permute-done.2.refs_2_.refs_12_), channel_id=1, source_target_pairs={{0,32},{32,64},{64,96},{96,128},{128,160},{160,192},{192,224},{224... | collective-permute-start | bytes 811016 | tf_op jit(solution)/shard_map/ppermute | solution.py:459
  17.8 6.8 %collective-permute-start.6 = (bf16[2,128,256]{2,1,0:T(8,128)(2,1)S(1)}, bf16[2,128,256]{2,1,0:T(8,128)(2,1)S(1)}, u32[]{:S(2)}, u32[]{:S(2)}) collective-permute-start(bf16[2,128,256]{2,1,0:T(8,128)(2,1)S(1)} %pad_maximum_fusion.2.refs_4_), channel_id=1, source_target_pairs={{0,32},{32,64},{64,96},{96,128},{128,160},{160,192},{192,224},{224... | collective-permute-start | bytes 393224 | tf_op jit(solution)/shard_map/ppermute | solution.py:459
  20.3 9.5 %collective-permute-start.16 = (bf16[2,512,128]{2,1,0:T(8,128)(2,1)}, bf16[2,512,128]{2,1,0:T(8,128)(2,1)}, u32[]{:S(2)}, u32[]{:S(2)}) collective-permute-start(bf16[2,512,128]{2,1,0:T(8,128)(2,1)} %collective-permute-done.14.refs_18_), channel_id=1, source_target_pairs={{0,32},{32,64},{64,96},{96,128},{128,160},{160,192},{192,224},{224... | collective-permute-start | bytes 786440 | tf_op jit(solution)/shard_map/ppermute | solution.py:459
  24.6 3.3 %collective-permute-start.7 = (bf16[2,128,256]{2,1,0:T(8,128)(2,1)S(1)}, bf16[2,128,256]{2,1,0:T(8,128)(2,1)S(1)}, u32[]{:S(2)}, u32[]{:S(2)}) collective-permute-start(bf16[2,128,256]{2,1,0:T(8,128)(2,1)S(1)} %collective-permute-done.6.refs_5_), channel_id=1, source_target_pairs={{0,16},{16,0},{32,48},{48,32},{64,80},{80,64},{96,112},{112,96},{1... | collective-permute-start | bytes 393224 | tf_op jit(solution)/shard_map/ppermute | solution.py:456
  24.6 7.3 %collective-permute-start.8 = (bf16[2,128,256]{2,1,0:T(8,128)(2,1)S(1)}, bf16[2,128,256]{2,1,0:T(8,128)(2,1)S(1)}, u32[]{:S(2)}, u32[]{:S(2)}) collective-permute-start(bf16[2,128,256]{2,1,0:T(8,128)(2,1)S(1)} %collective-permute-done.6.refs_5_), channel_id=1, source_target_pairs={{0,32},{32,64},{64,96},{96,128},{128,160},{160,192},{192,224},{224... | collective-permute-start | bytes 393224 | tf_op jit(solution)/shard_map/ppermute | solution.py:459
  25.9 0.7 copy-start.10
  26.6 7.9 %collective-permute-start.11 = (bf16[2,528,128]{2,1,0:T(8,128)(2,1)S(1)}, bf16[2,528,128]{2,1,0:T(8,128)(2,1)S(1)}, u32[]{:S(2)}, u32[]{:S(2)}) collective-permute-start(bf16[2,528,128]{2,1,0:T(8,128)(2,1)S(1)} %collective-permute-done.1.refs_2_.refs_10_), channel_id=1, source_target_pairs={{0,16},{16,0},{32,48},{48,32},{64,80},{80,64},{96,112},{112,96},{1... | collective-permute-start | bytes 811016 | tf_op jit(solution)/shard_map/ppermute | solution.py:456
  27.9 0.7 copy-start.12
  28.5 9.1 %collective-permute-start.10 = (bf16[2,528,128]{2,1,0:T(8,128)(2,1)S(1)}, bf16[2,528,128]{2,1,0:T(8,128)(2,1)S(1)}, u32[]{:S(2)}, u32[]{:S(2)}) collective-permute-start(bf16[2,528,128]{2,1,0:T(8,128)(2,1)S(1)} %collective-permute-done.2.refs_2_.refs_12_), channel_id=1, source_target_pairs={{0,16},{16,0},{32,48},{48,32},{64,80},{80,64},{96,112},{112,96},{1... | collective-permute-start | bytes 811016 | tf_op jit(solution)/shard_map/ppermute | solution.py:456
  28.6 0.7 copy-start
  29.3 9.6 %collective-permute-start.4 = (bf16[2,528,128]{2,1,0:T(8,128)(2,1)}, bf16[2,528,128]{2,1,0:T(8,128)(2,1)S(1)}, u32[]{:S(2)}, u32[]{:S(2)}) collective-permute-start(bf16[2,528,128]{2,1,0:T(8,128)(2,1)} %collective-permute-done.3.refs_2_.refs_14_), channel_id=1, source_target_pairs={{0,16},{16,0},{32,48},{48,32},{64,80},{80,64},{96,112},{112,96},{1... | collective-permute-start | bytes 811016 | tf_op jit(solution)/shard_map/ppermute | solution.py:456
  29.8 7.9 %collective-permute-start.18 = (bf16[2,512,128]{2,1,0:T(8,128)(2,1)}, bf16[2,512,128]{2,1,0:T(8,128)(2,1)}, u32[]{:S(2)}, u32[]{:S(2)}) collective-permute-start(bf16[2,512,128]{2,1,0:T(8,128)(2,1)} %collective-permute-done.16.refs_20_), channel_id=1, source_target_pairs={{0,32},{32,64},{64,96},{96,128},{128,160},{160,192},{192,224},{224... | collective-permute-start | bytes 786440 | tf_op jit(solution)/shard_map/ppermute | solution.py:459
  31.9 1.9 %collective-permute-start.9 = (bf16[2,128,256]{2,1,0:T(8,128)(2,1)S(1)}, bf16[2,128,256]{2,1,0:T(8,128)(2,1)S(1)}, u32[]{:S(2)}, u32[]{:S(2)}) collective-permute-start(bf16[2,128,256]{2,1,0:T(8,128)(2,1)S(1)} %collective-permute-done.8.refs_7_), channel_id=1, source_target_pairs={{0,16},{16,0},{32,48},{48,32},{64,80},{80,64},{96,112},{112,96},{1... | collective-permute-start | bytes 393224 | tf_op jit(solution)/shard_map/ppermute | solution.py:456
  32.8 0.6 copy-start.14
  33.8 0.6 copy-start.16
  34.4 18.4 %collective-permute-start.12 = (bf16[2,528,128]{2,1,0:T(8,128)(2,1)}, bf16[2,528,128]{2,1,0:T(8,128)(2,1)}, u32[]{:S(2)}, u32[]{:S(2)}) collective-permute-start(bf16[2,528,128]{2,1,0:T(8,128)(2,1)} %collective-permute-done.3.refs_2_.refs_14_), channel_id=1, source_target_pairs={{0,32},{32,64},{64,96},{96,128},{128,160},{160,192},{192,224},{224... | collective-permute-start | bytes 811016 | tf_op jit(solution)/shard_map/ppermute | solution.py:459
  34.5 0.7 copy-start.2
  35.2 19.8 %collective-permute-start.15 = (bf16[2,512,128]{2,1,0:T(8,128)(2,1)}, bf16[2,512,128]{2,1,0:T(8,128)(2,1)}, u32[]{:S(2)}, u32[]{:S(2)}) collective-permute-start(bf16[2,512,128]{2,1,0:T(8,128)(2,1)} %collective-permute-done.14.refs_18_), channel_id=1, source_target_pairs={{0,16},{16,0},{32,48},{48,32},{64,80},{80,64},{96,112},{112,96},{1... | collective-permute-start | bytes 786440 | tf_op jit(solution)/shard_map/ppermute | solution.py:456
  37.7 17.3 %collective-permute-start.17 = (bf16[2,512,128]{2,1,0:T(8,128)(2,1)}, bf16[2,512,128]{2,1,0:T(8,128)(2,1)}, u32[]{:S(2)}, u32[]{:S(2)}) collective-permute-start(bf16[2,512,128]{2,1,0:T(8,128)(2,1)} %collective-permute-done.16.refs_20_), channel_id=1, source_target_pairs={{0,16},{16,0},{32,48},{48,32},{64,80},{80,64},{96,112},{112,96},{1... | collective-permute-start | bytes 786440 | tf_op jit(solution)/shard_map/ppermute | solution.py:456
  37.7 0.7 copy-start.4
  38.4 16.6 %collective-permute-start.19 = (bf16[2,512,128]{2,1,0:T(8,128)(2,1)}, bf16[2,512,128]{2,1,0:T(8,128)(2,1)}, u32[]{:S(2)}, u32[]{:S(2)}) collective-permute-start(bf16[2,512,128]{2,1,0:T(8,128)(2,1)} %collective-permute-done.18.refs_22_), channel_id=1, source_target_pairs={{0,16},{16,0},{32,48},{48,32},{64,80},{80,64},{96,112},{112,96},{1... | collective-permute-start | bytes 786440 | tf_op jit(solution)/shard_map/ppermute | solution.py:456
  38.9 0.7 copy-start.6
  39.6 15.4 %collective-permute-start.20 = (bf16[2,512,128]{2,1,0:T(8,128)(2,1)}, bf16[2,512,128]{2,1,0:T(8,128)(2,1)}, u32[]{:S(2)}, u32[]{:S(2)}) collective-permute-start(bf16[2,512,128]{2,1,0:T(8,128)(2,1)} %collective-permute-done.18.refs_22_), channel_id=1, source_target_pairs={{0,32},{32,64},{64,96},{96,128},{128,160},{160,192},{192,224},{224... | collective-permute-start | bytes 786440 | tf_op jit(solution)/shard_map/ppermute | solution.py:459
  40.5 0.9 %copy-start.18 = (bf16[128,640]{1,0:T(8,128)(2,1)S(1)}, bf16[128,640]{1,0:T(8,128)(2,1)}, u32[]{:S(2)}) copy-start(bf16[128,640]{1,0:T(8,128)(2,1)} %refs_1_.1) | copy-start | bytes 491524
  41.4 0.9 %copy-start.19 = (bf16[128,640]{1,0:T(8,128)(2,1)S(1)}, bf16[128,640]{1,0:T(8,128)(2,1)}, u32[]{:S(2)}) copy-start(bf16[128,640]{1,0:T(8,128)(2,1)} %refs_2_.1) | copy-start | bytes 491524
  43.5 1.0 %copy-start.3 = (bf16[2,528,128]{2,1,0:T(8,128)(2,1)S(1)}, bf16[2,528,128]{2,1,0:T(8,128)(2,1)}, u32[]{:S(2)}) copy-start(bf16[2,528,128]{2,1,0:T(8,128)(2,1)} %copy-done.2) | copy-start | bytes 811012
  44.5 2.2 %copy-start.1 = (bf16[2,528,128]{2,1,0:T(8,128)(2,1)S(1)}, bf16[2,528,128]{2,1,0:T(8,128)(2,1)}, u32[]{:S(2)}) copy-start(bf16[2,528,128]{2,1,0:T(8,128)(2,1)} %copy-done) | copy-start | bytes 811012
  44.5 2.2 %copy-start.5 = (bf16[2,528,128]{2,1,0:T(8,128)(2,1)S(1)}, bf16[2,528,128]{2,1,0:T(8,128)(2,1)}, u32[]{:S(2)}) copy-start(bf16[2,528,128]{2,1,0:T(8,128)(2,1)} %copy-done.4) | copy-start | bytes 811012
  46.7 2.3 %copy-start.7 = (bf16[2,528,128]{2,1,0:T(8,128)(2,1)S(1)}, bf16[2,528,128]{2,1,0:T(8,128)(2,1)}, u32[]{:S(2)}) copy-start(bf16[2,528,128]{2,1,0:T(8,128)(2,1)} %copy-done.6) | copy-start | bytes 811012
  46.7 2.3 %copy-start.11 = (bf16[2,128,256]{2,1,0:T(8,128)(2,1)S(1)}, bf16[2,128,256]{2,1,0:T(8,128)(2,1)}, u32[]{:S(2)}) copy-start(bf16[2,128,256]{2,1,0:T(8,128)(2,1)} %copy-done.10) | copy-start | bytes 393220
  46.7 2.3 %copy-start.13 = (bf16[2,128,256]{2,1,0:T(8,128)(2,1)S(1)}, bf16[2,128,256]{2,1,0:T(8,128)(2,1)}, u32[]{:S(2)}) copy-start(bf16[2,128,256]{2,1,0:T(8,128)(2,1)} %copy-done.12) | copy-start | bytes 393220
  46.7 2.3 %copy-start.15 = (bf16[2,128,256]{2,1,0:T(8,128)(2,1)S(1)}, bf16[2,128,256]{2,1,0:T(8,128)(2,1)}, u32[]{:S(2)}) copy-start(bf16[2,128,256]{2,1,0:T(8,128)(2,1)} %copy-done.14) | copy-start | bytes 393220
  46.7 2.3 %copy-start.17 = (bf16[2,128,256]{2,1,0:T(8,128)(2,1)S(1)}, bf16[2,128,256]{2,1,0:T(8,128)(2,1)}, u32[]{:S(2)}) copy-start(bf16[2,128,256]{2,1,0:T(8,128)(2,1)} %copy-done.16) | copy-start | bytes 393220
  52.9 2.2 %copy-start.9 = (bf16[2,512,128]{2,1,0:T(8,128)(2,1)S(1)}, bf16[2,512,128]{2,1,0:T(8,128)(2,1)}, u32[]{:S(2)}) copy-start(bf16[2,512,128]{2,1,0:T(8,128)(2,1)} %copy-done.8) | copy-start | bytes 786436
  63.8 22.4 %collective-permute-start.21 = (bf16[128,256]{1,0:T(8,128)(2,1)S(1)}, bf16[128,256]{1,0:T(8,128)(2,1)S(1)}, u32[]{:S(2)}, u32[]{:S(2)}) collective-permute-start(bf16[128,256]{1,0:T(8,128)(2,1)S(1)} %get-tuple-element.74), channel_id=1, source_target_pairs={{16,0},{32,16},{48,32},{64,48},{80,64},{96,80},{112,96},{128,112},... | collective-permute-start | bytes 196616 | tf_op jit(solution)/shard_map/ppermute | solution.py:492
  67.8 18.4 %collective-permute-start.22 = (bf16[128,256]{1,0:T(8,128)(2,1)S(1)}, bf16[128,256]{1,0:T(8,128)(2,1)S(1)}, u32[]{:S(2)}, u32[]{:S(2)}) collective-permute-start(bf16[128,256]{1,0:T(8,128)(2,1)S(1)} %get-tuple-element.75), channel_id=1, source_target_pairs={{32,0},{48,16},{64,32},{80,48},{96,64},{112,80},{128,96},{144,112}... | collective-permute-start | bytes 196616 | tf_op jit(solution)/shard_map/ppermute | solution.py:492
  71.6 14.6 %collective-permute-start.23 = (bf16[128,256]{1,0:T(8,128)(2,1)S(1)}, bf16[128,256]{1,0:T(8,128)(2,1)S(1)}, u32[]{:S(2)}, u32[]{:S(2)}) collective-permute-start(bf16[128,256]{1,0:T(8,128)(2,1)S(1)} %get-tuple-element.76), channel_id=1, source_target_pairs={{48,0},{64,16},{80,32},{96,48},{112,64},{128,80},{144,96},{160,112... | collective-permute-start | bytes 196616 | tf_op jit(solution)/shard_map/ppermute | solution.py:492
  74.8 11.4 %collective-permute-start.24 = (bf16[128,256]{1,0:T(8,128)(2,1)S(1)}, bf16[128,256]{1,0:T(8,128)(2,1)S(1)}, u32[]{:S(2)}, u32[]{:S(2)}) collective-permute-start(bf16[128,256]{1,0:T(8,128)(2,1)S(1)} %get-tuple-element.77), channel_id=1, source_target_pairs={{64,0},{80,16},{96,32},{112,48},{128,64},{144,80},{160,96},{176,11... | collective-permute-start | bytes 196616 | tf_op jit(solution)/shard_map/ppermute | solution.py:492
where the time goes:
time: 88.4 us; the launch traced here: 86.9 us
  Pallas kernels  30.2 us (34%)
  starting transfers between devices  29.1 us (33%)
  waiting for transfers between devices  15.1 us (17%)
  local copies, waits for them, and re-layouts  8.24 us (9%)
  other arithmetic  3.37 us (4%)
  between operations  0.96 us (1%)
    ppermute x10, waiting for transfers between devices, turn(): return lax.ppermute(block, 'seq', ring)  13.4 us
    ppermute x4, starting transfers between devices, local(): returned.append(lax.ppermute(back[rim - distance], 'seq', route))  13.1 us
    ppermute x10, starting transfers between devices, turn(): return lax.ppermute(block, 'seq', ring)  11.7 us
    pallas_call x5, Pallas kernels, stats(): pl.pallas_call(functools.partial(stats_kernel, rows=rows, tile=tile, star...  11.5 us
    pallas_call x2, Pallas kernels, grad_stage(): pl.pallas_call(functools.partial(grad_kernel, rows=rows, span=span, last=...  9.27 us
    pallas_call x1, Pallas kernels, value_stage(): pl.pallas_call(functools.partial(value_kernel, rows=rows, tile=tile, coun...  8.73 us
    unnamed x40, local copies, waits for them, and re-layouts  8.24 us
    ppermute x11, starting transfers between devices, swap(): return lax.ppermute(block, 'seq', partner)  4.29 us
  transfers between devices with their start and end apart: 25, of which 6 were waited for; matrix products, arithmetic and copies ran while one was open for 2% of the time, Pallas kernels for 24%

commit v1 on v0

--- a/solution.py
+++ b/solution.py
@@ -226,14 +226,25 @@
 
 def value_kernel(*refs, rows, tile, counts):
     n = len(counts)
-    (queries, grads, window_ref, max_in, sum_in, raised, level, self_raised, self_level) = refs[:9]
-    key_packets = refs[9 : 9 + n]
-    value_packets = refs[9 + n : 9 + 2 * n]
-    outs = refs[9 + 2 * n :]
-    (attended_ref, factor_ref, delta, partial_ref, keys, values, own_ref) = outs[:7]
-    rim = window_ref.shape[0] // rows - 1
-    back_refs = outs[7 : 7 + rim]
-    (top_ref, inverse_ref, summed, self_weights, key_sems, value_sems) = outs[7 + rim :]
+    meta_ref = refs[0]
+    (queries, grads, window_ref, max_in, sum_in, raised, level, self_raised, self_level) = refs[1:10]
+    key_packets = refs[10 : 10 + n]
+    value_packets = refs[10 + n : 10 + 2 * n]
+    outs = refs[10 + 2 * n :]
+    (attended_ref, factor_ref, delta, partial_ref, keys, values, own_ref, give_ref, keep_ref) = outs[:9]
+    (top_ref, inverse_ref, summed, self_weights, key_sems, value_sems) = outs[9:]
+    even = meta_ref[0] % 2 == 0
+
+    def hand_out(grad, cs):
+        four, three, two, one, own = (grad[at, :] for at in cuts(window, rows))
+        nothing = jnp.zeros_like(own)
+        own_ref[:, cs] = own
+        give_ref[0, :, cs] = jnp.where(even, three, two).astype(jnp.bfloat16)
+        give_ref[1, :, cs] = jnp.where(even, four, three).astype(jnp.bfloat16)
+        give_ref[2, :, cs] = jnp.where(even, nothing, one).astype(jnp.bfloat16)
+        keep_ref[0, :, cs] = jnp.where(even, one, four)
+        keep_ref[1, :, cs] = jnp.where(even, two, nothing)
+
     copies = fetch_all(value_packets, counts, values, value_sems, tile)
     key_copies = fetch_all(key_packets, counts, keys, key_sems, tile)
     total = rows * GROUP
@@ -243,7 +254,6 @@
     cols = cuts(GROUP * HD, HD)
     lanes = cuts(tile, LANES)
     self_lanes = cuts(window, LANES)
-    first = window - rows
     for hs in heads:
         best = max_in[hs, :]
         top = jnp.max(best, axis=1, keepdims=True)
@@ -263,10 +273,7 @@
         parts.append(jnp.concatenate(pieces, axis=1))
     rounded = jnp.concatenate(parts, axis=0)
     summed[...] = nn(rounded, window_ref[:, HD:])
-    value_grads = tn(rounded, grads[...])
-    own_ref[:, HD:] = value_grads[first:, :]
-    for d, back_ref in enumerate(back_refs):
-        back_ref[:, HD:] = value_grads[d * rows : (d + 1) * rows, :].astype(jnp.bfloat16)
+    hand_out(tn(rounded, grads[...]), slice(HD, 2 * HD))
     for copy in copies:
         copy.wait()
 
@@ -298,10 +305,7 @@
         parts.append(jnp.concatenate(pieces, axis=1))
     grad_scores = jnp.concatenate(parts, axis=0)
     partial_ref[...] = nn(grad_scores, window_ref[:, :HD])
-    key_grads = tn(grad_scores, queries[...])
-    own_ref[:, :HD] = key_grads[first:, :]
-    for d, back_ref in enumerate(back_refs):
-        back_ref[:, :HD] = key_grads[d * rows : (d + 1) * rows, :].astype(jnp.bfloat16)
+    hand_out(tn(grad_scores, queries[...]), slice(0, HD))
     for copy in key_copies:
         copy.wait()
 
@@ -335,24 +339,28 @@
             out_ref[:, cs] = (summed[hs, :] * SCALE).astype(jnp.bfloat16)
 
 
-def combine_kernel(own_ref, *refs):
-    total = own_ref[...]
-    for ref in refs[:-2]:
-        total = total + ref[...].astype(jnp.float32)
-    refs[-2][...] = (total[:, :HD] * SCALE).astype(jnp.bfloat16)
-    refs[-1][...] = total[:, HD:].astype(jnp.bfloat16)
-
-
-def value_stage(queries, grads, window, state, key_packets, value_packets, rows, tile):
+def merge_kernel(keep_ref, swapped_ref, out_ref):
+    for n in range(2):
+        out_ref[n] = (keep_ref[n] + swapped_ref[n].astype(jnp.float32)).astype(jnp.bfloat16)
+
+
+def combine_kernel(meta_ref, own_ref, swapped_ref, near_ref, far_ref, keys_ref, values_ref):
+    mine = 1 - meta_ref[0] % 2
+    total = own_ref[...] + swapped_ref[2].astype(jnp.float32)
+    total = total + near_ref[mine].astype(jnp.float32) + far_ref[mine].astype(jnp.float32)
+    keys_ref[...] = (total[:, :HD] * SCALE).astype(jnp.bfloat16)
+    values_ref[...] = total[:, HD:].astype(jnp.bfloat16)
+
+
+def value_stage(my_index, queries, grads, window, state, key_packets, value_packets, rows, tile):
     counts = tuple(p.shape[0] for p in value_packets)
     tiles = sum(counts)
     total = rows * GROUP
     span = window.shape[0]
-    rim = span // rows - 1
     return pl.pallas_call(
         functools.partial(value_kernel, rows=rows, tile=tile, counts=counts),
-        in_specs=[WHOLE] * 9 + [ANYWHERE] * (2 * len(counts)),
-        out_specs=[WHOLE] * (7 + rim),
+        in_specs=[SCALARS] + [WHOLE] * 9 + [ANYWHERE] * (2 * len(counts)),
+        out_specs=[WHOLE] * 9,
         out_shape=[
             bf16(rows, GROUP * HD),
             f32(tiles, total, LANES),
@@ -361,8 +369,9 @@
             bf16(tiles, tile, HD),
             bf16(tiles, tile, HD),
             f32(rows, 2 * HD),
-        ]
-        + [bf16(rows, 2 * HD)] * rim,
+            bf16(3, rows, 2 * HD),
+            f32(2, rows, 2 * HD),
+        ],
         scratch_shapes=[
             pltpu.VMEM((total, LANES), jnp.float32),
             pltpu.VMEM((total, LANES), jnp.float32),
@@ -371,13 +380,13 @@
             pltpu.SemaphoreType.DMA((len(counts),)),
             pltpu.SemaphoreType.DMA((len(counts),)),
         ],
-        input_output_aliases={6: 1},
+        input_output_aliases={7: 1},
         compiler_params=LIMIT,
         cost_estimate=pl.CostEstimate(
             flops=2 * total * HD * tiles * tile, transcendentals=0, bytes_accessed=tiles * tile * HD
         ),
         name="value_stage",
-    )(queries, grads, window, *state, *key_packets, *value_packets)
+    )(my_index, queries, grads, window, *state, *key_packets, *value_packets)
 
 
 def grad_stage(grads, raised, factor, delta, partial, keys, values, rows, span, last):
@@ -399,16 +408,27 @@
     )(grads, raised, factor, delta, partial, keys, values)
 
 
-def combine(own, returned):
+def merge(keep, swapped):
+    return pl.pallas_call(
+        merge_kernel,
+        in_specs=[WHOLE] * 2,
+        out_specs=WHOLE,
+        out_shape=bf16(*keep.shape),
+        compiler_params=LIMIT,
+        name="merge",
+    )(keep, swapped)
+
+
+def combine(my_index, own, swapped, near, far):
     rows = own.shape[0]
     return pl.pallas_call(
         combine_kernel,
-        in_specs=[WHOLE] * (1 + len(returned)),
+        in_specs=[SCALARS] + [WHOLE] * 4,
         out_specs=[WHOLE] * 2,
         out_shape=[bf16(rows, HD)] * 2,
         compiler_params=LIMIT,
         name="combine",
-    )(own, *returned)
+    )(my_index, own, swapped, near, far)
 
 
 def compute(index, query, d_out, key_groups, value_groups, selfs, selfs_at, shape):
@@ -427,8 +447,8 @@
         done += sum(p.shape[0] for p in group)
     key_packets = [p for group in key_groups for p in group]
     value_packets = [p for group in value_groups for p in group]
-    attended, factor, delta, partial, keys, values, own, *back = value_stage(
-        queries, grads, window, [*state, *self_state], key_packets, value_packets, rows, tile
+    attended, factor, delta, partial, keys, values, own, give, keep = value_stage(
+        index, queries, grads, window, [*state, *self_state], key_packets, value_packets, rows, tile
     )
 
     def finish():
@@ -436,7 +456,7 @@
         summed = grad_stage(*shared, partial, keys, values, rows, (0, tiles // 2), False)
         return grad_stage(*shared, summed, keys, values, rows, (tiles // 2, tiles), True)
 
-    return attended, finish, own, back
+    return attended, finish, own, give, keep
 
 
 def local(query, self_keys, self_values, cache_keys, cache_values, cache_pos, d_out):
@@ -445,7 +465,6 @@
     peers = lax.axis_size("seq")
     my_index = lax.axis_index("seq")
     start_pos = (tile - rows) * peers
-    rim = (WINDOW + rows - 2) // rows
     chips = peers // 2
 
     partner = [(i, i ^ 1) for i in range(peers)]
@@ -483,15 +502,16 @@
             selfs += [self_block, swap(self_block)]
 
     index = my_index.reshape(1)
-    attended, finish, own, back = compute(
+    attended, finish, own, give, keep = compute(
         index, query, d_out, key_groups, value_groups, selfs, 3, (rows, tile, start_pos)
     )
-    returned = []
-    for distance in range(1, rim + 1):
-        route = [(i, i - distance) for i in range(distance, peers)]
-        returned.append(lax.ppermute(back[rim - distance], "seq", route))
+    back = [(2 * z, 2 * z - 2) for z in range(1, chips)]
+    back += [(2 * z + 1, 2 * z - 3) for z in range(2, chips)]
+    swapped = swap(give)
+    near = lax.ppermute(merge(keep, swapped), "seq", back)
+    far = swap(near)
     grad_query = finish()
-    grad_keys, grad_values = combine(own, returned)
+    grad_keys, grad_values = combine(index, own, swapped, near, far)
     return attended, grad_query, grad_keys, grad_values
 
 

time: 88.4 us -> 91.3 us (1.033)
  the two profiles are of different devices: /device:TPU:194 before, /device:TPU:1 now
where the time goes in v1:
time: 91.3 us; the launch traced here: 90.9 us
  Pallas kernels  30.7 us (34%)
  starting transfers between devices  29.1 us (32%)
  waiting for transfers between devices  18 us (20%)
  local copies, waits for them, and re-layouts  8.85 us (10%)
  other arithmetic  3.38 us (4%)
  between operations  0.97 us (1%)
    ppermute x10, starting transfers between devices, turn(): return lax.ppermute(block, 'seq', ring)  16.7 us
    pallas_call x5, Pallas kernels, stats(): pl.pallas_call(functools.partial(stats_kernel, rows=rows, tile=tile, star...  11.5 us
    ppermute x13, starting transfers between devices, swap(): return lax.ppermute(block, 'seq', partner)  11 us
    pallas_call x2, Pallas kernels, grad_stage(): pl.pallas_call(functools.partial(grad_kernel, rows=rows, span=span, last=...  9.47 us
    pallas_call x1, Pallas kernels, value_stage(): pl.pallas_call(functools.partial(value_kernel, rows=rows, tile=tile, coun...  8.99 us
    unnamed x44, local copies, waits for them, and re-layouts  8.85 us
    ppermute x1, waiting for transfers between devices, local(): near = lax.ppermute(merge(keep, swapped), 'seq', back)  7.82 us
    ppermute x10, waiting for transfers between devices, turn(): return lax.ppermute(block, 'seq', ring)  7.03 us
  transfers between devices with their start and end apart: 24, of which 9 were waited for; matrix products, arithmetic and copies ran while one was open for 2% of the time, Pallas kernels for 23%

profile of v1, /device:TPU:1, one launch (start us, length us, event | category | flops | bytes accessed | tf_op | source)
XLA Modules:
  0.0 90.9 jit_solution(13927645114353902806)
XLA Ops:
  0.6 0.7 fusion.7
  1.3 0.9 %maximum_bitcast_fusion = bf16[1,528,128]{2,1,0:T(8,128)(2,1)S(1)} fusion(bf16[16,128]{1,0:T(8,128)(2,1)S(1)} %fusion.2, bf16[512,128]{1,0:T(8,128)(2,1)} %param.10), kind=kLoop, calls=%fused_computation.2 | loop fusion | flops 270336 | bytes 270336 | tf_op jit(solution)/shard_map/broadcast_in_dim | solution.py:483
  2.3 3.3 %collective-permute-start = (bf16[1,528,128]{2,1,0:T(8,128)(2,1)S(1)}, bf16[1,528,128]{2,1,0:T(8,128)(2,1)S(1)}, u32[]{:S(2)}, u32[]{:S(2)}) collective-permute-start(bf16[1,528,128]{2,1,0:T(8,128)(2,1)S(1)} %maximum_bitcast_fusion), channel_id=1, source_target_pairs={{0,16},{16,0},{32,48},{48,32},{64,80},{80,64},{96,112},{112,96},{1... | collective-permute-start | bytes 405512 | tf_op jit(solution)/shard_map/ppermute | solution.py:475
  5.5 1.0 %collective-permute-done = bf16[1,528,128]{2,1,0:T(8,128)(2,1)S(1)} collective-permute-done((bf16[1,528,128]{2,1,0:T(8,128)(2,1)S(1)}, bf16[1,528,128]{2,1,0:T(8,128)(2,1)S(1)}, u32[]{:S(2)}, u32[]{:S(2)}) %collective-permute-start) | collective-permute-done | bytes 135200 | tf_op jit(solution)/shard_map/ppermute | solution.py:475
  6.6 3.9 %collective-permute-start.1 = (bf16[2,528,128]{2,1,0:T(8,128)(2,1)S(1)}, bf16[2,528,128]{2,1,0:T(8,128)(2,1)S(1)}, u32[]{:S(2)}, u32[]{:S(2)}) collective-permute-start(bf16[2,528,128]{2,1,0:T(8,128)(2,1)S(1)} %pad_maximum_fusion.refs_3_.refs_10_), channel_id=1, source_target_pairs={{0,32},{32,64},{64,96},{96,128},{128,160},{160,192},{192,224},{224... | collective-permute-start | bytes 811016 | tf_op jit(solution)/shard_map/ppermute | solution.py:478
  10.5 3.4 %collective-permute-done.1.refs_2_.refs_11_ = bf16[2,528,128]{2,1,0:T(8,128)(2,1)S(1)} collective-permute-done((bf16[2,528,128]{2,1,0:T(8,128)(2,1)S(1)}, bf16[2,528,128]{2,1,0:T(8,128)(2,1)S(1)}, u32[]{:S(2)}, u32[]{:S(2)}) %collective-permute-start.1) | collective-permute-done | bytes 270368 | tf_op jit(solution)/shard_map/ppermute | solution.py:478
  13.9 3.1 %collective-permute-start.2 = (bf16[2,528,128]{2,1,0:T(8,128)(2,1)S(1)}, bf16[2,528,128]{2,1,0:T(8,128)(2,1)S(1)}, u32[]{:S(2)}, u32[]{:S(2)}) collective-permute-start(bf16[2,528,128]{2,1,0:T(8,128)(2,1)S(1)} %collective-permute-done.1.refs_2_.refs_11_), channel_id=1, source_target_pairs={{0,32},{32,64},{64,96},{96,128},{128,160},{160,192},{192,224},{224... | collective-permute-start | bytes 811016 | tf_op jit(solution)/shard_map/ppermute | solution.py:478
  17.0 0.9 %pad_maximum_fusion.1.refs_18_ = bf16[2,512,128]{2,1,0:T(8,128)(2,1)S(1)} fusion(bf16[1,512,128]{2,1,0:T(8,128)(2,1)S(1)} %collective-permute-done.13, bf16[1,512,128]{2,1,0:T(8,128)(2,1)} %bitcast.11), kind=kLoop, calls=%fused_computation.1 | loop fusion | flops 131072 | bytes 524288 | tf_op jit(solution)/shard_map/concatenate | solution.py:487
  18.1 0.8 maximum_bitcast_fusion.1
  19.0 1.5 %collective-permute-done.2.refs_2_.refs_13_ = bf16[2,528,128]{2,1,0:T(8,128)(2,1)S(1)} collective-permute-done((bf16[2,528,128]{2,1,0:T(8,128)(2,1)S(1)}, bf16[2,528,128]{2,1,0:T(8,128)(2,1)S(1)}, u32[]{:S(2)}, u32[]{:S(2)}) %collective-permute-start.2) | collective-permute-done | bytes 270368 | tf_op jit(solution)/shard_map/ppermute | solution.py:478
  20.4 3.1 %collective-permute-start.3 = (bf16[2,528,128]{2,1,0:T(8,128)(2,1)S(1)}, bf16[2,528,128]{2,1,0:T(8,128)(2,1)}, u32[]{:S(2)}, u32[]{:S(2)}) collective-permute-start(bf16[2,528,128]{2,1,0:T(8,128)(2,1)S(1)} %collective-permute-done.2.refs_2_.refs_13_), channel_id=1, source_target_pairs={{0,32},{32,64},{64,96},{96,128},{128,160},{160,192},{192,224},{224... | collective-permute-start | bytes 811016 | tf_op jit(solution)/shard_map/ppermute | solution.py:478
  23.7 0.6 copy-done.10
  24.3 2.1 %collective-permute-start.16 = (bf16[2,512,128]{2,1,0:T(8,128)(2,1)}, bf16[2,512,128]{2,1,0:T(8,128)(2,1)}, u32[]{:S(2)}, u32[]{:S(2)}) collective-permute-start(bf16[2,512,128]{2,1,0:T(8,128)(2,1)} %collective-permute-done.14.refs_19_), channel_id=1, source_target_pairs={{0,32},{32,64},{64,96},{96,128},{128,160},{160,192},{192,224},{224... | collective-permute-start | bytes 786440 | tf_op jit(solution)/shard_map/ppermute | solution.py:478
  26.5 1.9 %collective-permute-done.6.refs_5_ = bf16[2,128,256]{2,1,0:T(8,128)(2,1)S(1)} collective-permute-done((bf16[2,128,256]{2,1,0:T(8,128)(2,1)S(1)}, bf16[2,128,256]{2,1,0:T(8,128)(2,1)S(1)}, u32[]{:S(2)}, u32[]{:S(2)}) %collective-permute-start.6) | collective-permute-done | bytes 131104 | tf_op jit(solution)/shard_map/ppermute | solution.py:478
  28.4 4.0 %collective-permute-start.7 = (bf16[2,128,256]{2,1,0:T(8,128)(2,1)S(1)}, bf16[2,128,256]{2,1,0:T(8,128)(2,1)S(1)}, u32[]{:S(2)}, u32[]{:S(2)}) collective-permute-start(bf16[2,128,256]{2,1,0:T(8,128)(2,1)S(1)} %collective-permute-done.6.refs_5_), channel_id=1, source_target_pairs={{0,16},{16,0},{32,48},{48,32},{64,80},{80,64},{96,112},{112,96},{1... | collective-permute-start | bytes 393224 | tf_op jit(solution)/shard_map/ppermute | solution.py:475
  32.3 0.7 copy-done.12
  33.0 0.3 collective-permute-done.7.refs_6_
  33.3 0.7 copy-done.14
  34.0 0.4 collective-permute-start.10
  34.3 0.7 copy-done
  35.0 0.1 collective-permute-start.4
  35.2 2.6 %collective-permute-start.18 = (bf16[2,512,128]{2,1,0:T(8,128)(2,1)}, bf16[2,512,128]{2,1,0:T(8,128)(2,1)}, u32[]{:S(2)}, u32[]{:S(2)}) collective-permute-start(bf16[2,512,128]{2,1,0:T(8,128)(2,1)} %collective-permute-done.16.refs_21_), channel_id=1, source_target_pairs={{0,32},{32,64},{64,96},{96,128},{128,160},{160,192},{192,224},{224... | collective-permute-start | bytes 786440 | tf_op jit(solution)/shard_map/ppermute | solution.py:478
  37.8 0.7 collective-permute-start.9
  38.5 0.6 copy-done.16
  39.2 0.3 collective-permute-done.9.refs_8_
  39.5 0.6 copy-done.18
  40.2 0.7 copy-done.2
  40.9 0.4 collective-permute-start.15
  41.2 0.2 collective-permute-done.18.refs_23_
  41.5 2.0 %collective-permute-start.17 = (bf16[2,512,128]{2,1,0:T(8,128)(2,1)}, bf16[2,512,128]{2,1,0:T(8,128)(2,1)}, u32[]{:S(2)}, u32[]{:S(2)}) collective-permute-start(bf16[2,512,128]{2,1,0:T(8,128)(2,1)} %collective-permute-done.16.refs_21_), channel_id=1, source_target_pairs={{0,16},{16,0},{32,48},{48,32},{64,80},{80,64},{96,112},{112,96},{1... | collective-permute-start | bytes 786440 | tf_op jit(solution)/shard_map/ppermute | solution.py:475
  43.5 0.7 copy-done.4
  44.2 0.7 copy-done.6
  44.9 1.6 %collective-permute-start.20 = (bf16[2,512,128]{2,1,0:T(8,128)(2,1)}, bf16[2,512,128]{2,1,0:T(8,128)(2,1)}, u32[]{:S(2)}, u32[]{:S(2)}) collective-permute-start(bf16[2,512,128]{2,1,0:T(8,128)(2,1)} %collective-permute-done.18.refs_23_), channel_id=1, source_target_pairs={{0,32},{32,64},{64,96},{96,128},{128,160},{160,192},{192,224},{224... | collective-permute-start | bytes 786440 | tf_op jit(solution)/shard_map/ppermute | solution.py:478
  46.5 0.9 %copy-done.20 = bf16[128,640]{1,0:T(8,128)(2,1)S(1)} copy-done((bf16[128,640]{1,0:T(8,128)(2,1)S(1)}, bf16[128,640]{1,0:T(8,128)(2,1)}, u32[]{:S(2)}) %copy-start.20) | copy-done | bytes 163864
  47.4 0.9 %copy-done.21 = bf16[128,640]{1,0:T(8,128)(2,1)S(1)} copy-done((bf16[128,640]{1,0:T(8,128)(2,1)S(1)}, bf16[128,640]{1,0:T(8,128)(2,1)}, u32[]{:S(2)}) %copy-start.21) | copy-done | bytes 163864
  48.3 1.2 %stats.5 = (f32[640,128]{1,0:T(8,128)S(1)}, f32[640,128]{1,0:T(8,128)S(1)}, f32[16,640,512]{2,1,0:T(8,128)S(1)}, f32[16,640,128]{2,1,0:T(8,128)S(1)}, bf16[640,1...) custom-call(s32[1]{0:T(128)} %bitcast.refs_0_.meta_ref, bf16[128,640]{1,0:T(8,128)(2,1)S(1)} %copy-done.20, ...), custom_call_target="tpu_custom_call" | custom-call | flops 167772160 | bytes 262144 | tf_op jit(solution)/shard_map/stats/pallas_call | solution.py:192
  49.5 0.9 %copy-done.3 = bf16[2,528,128]{2,1,0:T(8,128)(2,1)S(1)} copy-done((bf16[2,528,128]{2,1,0:T(8,128)(2,1)S(1)}, bf16[2,528,128]{2,1,0:T(8,128)(2,1)}, u32[]{:S(2)}) %copy-start.3) | copy-done | bytes 270360
  50.5 2.2 %stats.6 = (f32[640,128]{1,0:T(8,128)S(1)}, f32[640,128]{1,0:T(8,128)S(1)}, f32[16,640,512]{2,1,0:T(8,128)S(1)}, f32[16,640,128]{2,1,0:T(8,128)S(1)}) custom-call(s32[1]{0:T(128)} %bitcast.refs_0_.meta_ref, bf16[640,128]{1,0:T(8,128)(2,1)S(1)} %get-tuple-element.40.refs_1_, ...), custom_call_target="tpu_custom_call", output_to_operand_aliasing={{2}: (6, {}), {3}: (7, {})} | custom-call | flops 335544320 | bytes 524288 | tf_op jit(solution)/shard_map/stats/pallas_call | solution.py:192
  52.8 2.2 %stats.7 = (f32[640,128]{1,0:T(8,128)S(1)}, f32[640,128]{1,0:T(8,128)S(1)}, f32[16,640,512]{2,1,0:T(8,128)S(1)}, f32[16,640,128]{2,1,0:T(8,128)S(1)}) custom-call(s32[1]{0:T(128)} %bitcast.refs_0_.meta_ref, bf16[640,128]{1,0:T(8,128)(2,1)S(1)} %get-tuple-element.40.refs_1_, ...), custom_call_target="tpu_custom_call", output_to_operand_aliasing={{2}: (6, {}), {3}: (7, {})} | custom-call | flops 335544320 | bytes 524288 | tf_op jit(solution)/shard_map/stats/pallas_call | solution.py:192
  55.0 3.8 %stats.8 = (f32[640,128]{1,0:T(8,128)S(1)}, f32[640,128]{1,0:T(8,128)S(1)}, f32[16,640,512]{2,1,0:T(8,128)S(1)}, f32[16,640,128]{2,1,0:T(8,128)S(1)}, f32[640,64...) custom-call(s32[1]{0:T(128)} %bitcast.refs_0_.meta_ref, ...), custom_call_target="tpu_custom_call", output_to_operand_aliasing={{2}: (11, {}), {3}: (12, {})} | custom-call | flops 335544320 | bytes 524288 | tf_op jit(solution)/shard_map/stats/pallas_call | solution.py:192
  58.9 2.1 %stats.9 = (f32[640,128]{1,0:T(8,128)S(1)}, f32[640,128]{1,0:T(8,128)S(1)}, f32[16,640,512]{2,1,0:T(8,128)S(1)}, f32[16,640,128]{2,1,0:T(8,128)S(1)}) custom-call(s32[1]{0:T(128)} %bitcast.refs_0_.meta_ref, bf16[640,128]{1,0:T(8,128)(2,1)S(1)} %get-tuple-element.40.refs_1_, ...), custom_call_target="tpu_custom_call", output_to_operand_aliasing={{2}: (5, {}), {3}: (6, {})} | custom-call | flops 167772160 | bytes 262144 | tf_op jit(solution)/shard_map/stats/pallas_call | solution.py:192
  61.1 9.0 %value_stage.1 = (bf16[128,640]{1,0:T(8,128)(2,1)}, f32[16,640,128]{2,1,0:T(8,128)S(1)}, f32[640,128]{1,0:T(8,128)S(1)}, f32[640,128]{1,0:T(8,128)S(1)}, bf16[16...) custom-call(s32[1]{0:T(128)} %bitcast.refs_0_.meta_ref, ...), custom_call_target="tpu_custom_call", output_to_operand_aliasing={{1}: (7, {})} | custom-call | flops 1342177280 | bytes 1048576 | tf_op jit(solution)/shard_map/value_stage/pallas_call | solution.py:360
  70.2 1.4 %collective-permute-done.21.swapped_ref = bf16[3,128,256]{2,1,0:T(8,128)(2,1)S(1)} collective-permute-done((bf16[3,128,256]{2,1,0:T(8,128)(2,1)S(1)}, bf16[3,128,256]{2,1,0:T(8,128)(2,1)S(1)}, u32[]{:S(2)}, u32[]{:S(2)}) %collective-permute-start.21) | collective-permute-done | bytes 196640 | tf_op jit(solution)/shard_map/ppermute | solution.py:475
  71.6 1.3 %collective-permute-start.22 = (bf16[2,128,256]{2,1,0:T(8,128)(2,1)S(1)}, bf16[2,128,256]{2,1,0:T(8,128)(2,1)S(1)}, u32[]{:S(2)}, u32[]{:S(2)}) collective-permute-start(bf16[2,128,256]{2,1,0:T(8,128)(2,1)S(1)} %merge.1), channel_id=1, source_target_pairs={{32,0},{64,32},{96,64},{128,96},{160,128},{192,160},{224,192},{80,... | collective-permute-start | bytes 393224 | tf_op jit(solution)/shard_map/ppermute | solution.py:511
  72.9 7.8 %collective-permute-done.22.near_ref = bf16[2,128,256]{2,1,0:T(8,128)(2,1)S(1)} collective-permute-done((bf16[2,128,256]{2,1,0:T(8,128)(2,1)S(1)}, bf16[2,128,256]{2,1,0:T(8,128)(2,1)S(1)}, u32[]{:S(2)}, u32[]{:S(2)}) %collective-permute-start.22) | collective-permute-done | bytes 131104 | tf_op jit(solution)/shard_map/ppermute | solution.py:511
  80.8 4.4 %grad_stage.2.partial_ref = f32[640,128]{1,0:T(8,128)S(1)} custom-call(bf16[640,128]{1,0:T(8,128)(2,1)S(1)} %get-tuple-element.41.refs_2_.grads, f32[16,640,512]{2,1,0:T(8,128)S(1)} %get-tuple-element.61.refs_6_.raised, f32[16,640,128]{2,1,0:T(8,128)S(1)} %get-tuple-element.66.factor_ref, f32[640,128]{1,0:T(8,128)S(1)} %get-tuple-element.67.delta, ...), custom_call_target="tpu_custom_call" | custom-call | flops 1342177280 | bytes 1048576 | tf_op jit(solution)/shard_map/grad_stage/pallas_call | solution.py:395
  85.2 5.1 %grad_stage.3 = bf16[128,640]{1,0:T(8,128)(2,1)} custom-call(bf16[640,128]{1,0:T(8,128)(2,1)S(1)} %get-tuple-element.41.refs_2_.grads, f32[16,640,512]{2,1,0:T(8,128)S(1)} %get-tuple-element.61.refs_6_.raised, f32[16,640,128]{2,1,0:T(8,128)S(1)} %get-tuple-element.66.factor_ref, f32[640,128]{1,0:T(8,128)S(1)} %get-tuple-element.67.delta, ...), custom_call_target="tpu_custom_call" | custom-call | flops 1342177280 | bytes 1048576 | tf_op jit(solution)/shard_map/grad_stage/pallas_call | solution.py:395
  90.2 0.7 combine.1
  (61 shorter events, 0.6 us)
Async XLA Ops:
  2.3 4.3 %collective-permute-start = (bf16[1,528,128]{2,1,0:T(8,128)(2,1)S(1)}, bf16[1,528,128]{2,1,0:T(8,128)(2,1)S(1)}, u32[]{:S(2)}, u32[]{:S(2)}) collective-permute-start(bf16[1,528,128]{2,1,0:T(8,128)(2,1)S(1)} %maximum_bitcast_fusion), channel_id=1, source_target_pairs={{0,16},{16,0},{32,48},{48,32},{64,80},{80,64},{96,112},{112,96},{1... | collective-permute-start | bytes 405512 | tf_op jit(solution)/shard_map/ppermute | solution.py:475
  6.6 7.3 %collective-permute-start.1 = (bf16[2,528,128]{2,1,0:T(8,128)(2,1)S(1)}, bf16[2,528,128]{2,1,0:T(8,128)(2,1)S(1)}, u32[]{:S(2)}, u32[]{:S(2)}) collective-permute-start(bf16[2,528,128]{2,1,0:T(8,128)(2,1)S(1)} %pad_maximum_fusion.refs_3_.refs_10_), channel_id=1, source_target_pairs={{0,32},{32,64},{64,96},{96,128},{128,160},{160,192},{192,224},{224... | collective-permute-start | bytes 811016 | tf_op jit(solution)/shard_map/ppermute | solution.py:478
  10.5 6.5 %collective-permute-start.13 = (bf16[1,512,128]{2,1,0:T(8,128)(2,1)}, bf16[1,512,128]{2,1,0:T(8,128)(2,1)S(1)}, u32[]{:S(2)}, u32[]{:S(2)}) collective-permute-start(bf16[1,512,128]{2,1,0:T(8,128)(2,1)} %bitcast.10), channel_id=1, source_target_pairs={{0,16},{16,0},{32,48},{48,32},{64,80},{80,64},{96,112},{112,96},{1... | collective-permute-start | bytes 393224 | tf_op jit(solution)/shard_map/ppermute | solution.py:475
  13.9 6.5 %collective-permute-start.2 = (bf16[2,528,128]{2,1,0:T(8,128)(2,1)S(1)}, bf16[2,528,128]{2,1,0:T(8,128)(2,1)S(1)}, u32[]{:S(2)}, u32[]{:S(2)}) collective-permute-start(bf16[2,528,128]{2,1,0:T(8,128)(2,1)S(1)} %collective-permute-done.1.refs_2_.refs_11_), channel_id=1, source_target_pairs={{0,32},{32,64},{64,96},{96,128},{128,160},{160,192},{192,224},{224... | collective-permute-start | bytes 811016 | tf_op jit(solution)/shard_map/ppermute | solution.py:478
  18.0 26.2 %copy-start.8 = (bf16[2,512,128]{2,1,0:T(8,128)(2,1)}, bf16[2,512,128]{2,1,0:T(8,128)(2,1)S(1)}, u32[]{:S(2)}) copy-start(bf16[2,512,128]{2,1,0:T(8,128)(2,1)S(1)} %pad_maximum_fusion.1.refs_18_) | copy-start | bytes 786436
  18.0 6.3 %collective-permute-start.14 = (bf16[2,512,128]{2,1,0:T(8,128)(2,1)S(1)}, bf16[2,512,128]{2,1,0:T(8,128)(2,1)}, u32[]{:S(2)}, u32[]{:S(2)}) collective-permute-start(bf16[2,512,128]{2,1,0:T(8,128)(2,1)S(1)} %pad_maximum_fusion.1.refs_18_), channel_id=1, source_target_pairs={{0,32},{32,64},{64,96},{96,128},{128,160},{160,192},{192,224},{224... | collective-permute-start | bytes 786440 | tf_op jit(solution)/shard_map/ppermute | solution.py:478
  18.9 4.7 %collective-permute-start.5 = (bf16[1,128,256]{2,1,0:T(8,128)(2,1)S(1)}, bf16[1,128,256]{2,1,0:T(8,128)(2,1)S(1)}, u32[]{:S(2)}, u32[]{:S(2)}) collective-permute-start(bf16[1,128,256]{2,1,0:T(8,128)(2,1)S(1)} %maximum_bitcast_fusion.1), channel_id=1, source_target_pairs={{0,16},{16,0},{32,48},{48,32},{64,80},{80,64},{96,112},{112,96},{1... | collective-permute-start | bytes 196616 | tf_op jit(solution)/shard_map/ppermute | solution.py:475
  20.4 14.6 %collective-permute-start.3 = (bf16[2,528,128]{2,1,0:T(8,128)(2,1)S(1)}, bf16[2,528,128]{2,1,0:T(8,128)(2,1)}, u32[]{:S(2)}, u32[]{:S(2)}) collective-permute-start(bf16[2,528,128]{2,1,0:T(8,128)(2,1)S(1)} %collective-permute-done.2.refs_2_.refs_13_), channel_id=1, source_target_pairs={{0,32},{32,64},{64,96},{96,128},{128,160},{160,192},{192,224},{224... | collective-permute-start | bytes 811016 | tf_op jit(solution)/shard_map/ppermute | solution.py:478
  23.6 4.8 %collective-permute-start.6 = (bf16[2,128,256]{2,1,0:T(8,128)(2,1)S(1)}, bf16[2,128,256]{2,1,0:T(8,128)(2,1)S(1)}, u32[]{:S(2)}, u32[]{:S(2)}) collective-permute-start(bf16[2,128,256]{2,1,0:T(8,128)(2,1)S(1)} %pad_maximum_fusion.2.refs_4_), channel_id=1, source_target_pairs={{0,32},{32,64},{64,96},{96,128},{128,160},{160,192},{192,224},{224... | collective-permute-start | bytes 393224 | tf_op jit(solution)/shard_map/ppermute | solution.py:478
  23.7 0.7 copy-start.10
  24.3 10.9 %collective-permute-start.16 = (bf16[2,512,128]{2,1,0:T(8,128)(2,1)}, bf16[2,512,128]{2,1,0:T(8,128)(2,1)}, u32[]{:S(2)}, u32[]{:S(2)}) collective-permute-start(bf16[2,512,128]{2,1,0:T(8,128)(2,1)} %collective-permute-done.14.refs_19_), channel_id=1, source_target_pairs={{0,32},{32,64},{64,96},{96,128},{128,160},{160,192},{192,224},{224... | collective-permute-start | bytes 786440 | tf_op jit(solution)/shard_map/ppermute | solution.py:478
  28.4 5.0 %collective-permute-start.7 = (bf16[2,128,256]{2,1,0:T(8,128)(2,1)S(1)}, bf16[2,128,256]{2,1,0:T(8,128)(2,1)S(1)}, u32[]{:S(2)}, u32[]{:S(2)}) collective-permute-start(bf16[2,128,256]{2,1,0:T(8,128)(2,1)S(1)} %collective-permute-done.6.refs_5_), channel_id=1, source_target_pairs={{0,16},{16,0},{32,48},{48,32},{64,80},{80,64},{96,112},{112,96},{1... | collective-permute-start | bytes 393224 | tf_op jit(solution)/shard_map/ppermute | solution.py:475
  32.3 5.5 %collective-permute-start.8 = (bf16[2,128,256]{2,1,0:T(8,128)(2,1)S(1)}, bf16[2,128,256]{2,1,0:T(8,128)(2,1)S(1)}, u32[]{:S(2)}, u32[]{:S(2)}) collective-permute-start(bf16[2,128,256]{2,1,0:T(8,128)(2,1)S(1)} %collective-permute-done.6.refs_5_), channel_id=1, source_target_pairs={{0,32},{32,64},{64,96},{96,128},{128,160},{160,192},{192,224},{224... | collective-permute-start | bytes 393224 | tf_op jit(solution)/shard_map/ppermute | solution.py:478
  32.3 0.7 copy-start.12
  33.0 7.2 %collective-permute-start.11 = (bf16[2,528,128]{2,1,0:T(8,128)(2,1)S(1)}, bf16[2,528,128]{2,1,0:T(8,128)(2,1)S(1)}, u32[]{:S(2)}, u32[]{:S(2)}) collective-permute-start(bf16[2,528,128]{2,1,0:T(8,128)(2,1)S(1)} %collective-permute-done.1.refs_2_.refs_11_), channel_id=1, source_target_pairs={{0,16},{16,0},{32,48},{48,32},{64,80},{80,64},{96,112},{112,96},{1... | collective-permute-start | bytes 811016 | tf_op jit(solution)/shard_map/ppermute | solution.py:475
  33.3 0.7 copy-start.14
  34.0 9.5 %collective-permute-start.10 = (bf16[2,528,128]{2,1,0:T(8,128)(2,1)S(1)}, bf16[2,528,128]{2,1,0:T(8,128)(2,1)S(1)}, u32[]{:S(2)}, u32[]{:S(2)}) collective-permute-start(bf16[2,528,128]{2,1,0:T(8,128)(2,1)S(1)} %collective-permute-done.2.refs_2_.refs_13_), channel_id=1, source_target_pairs={{0,16},{16,0},{32,48},{48,32},{64,80},{80,64},{96,112},{112,96},{1... | collective-permute-start | bytes 811016 | tf_op jit(solution)/shard_map/ppermute | solution.py:475
  34.3 0.7 copy-start
  35.0 9.1 %collective-permute-start.4 = (bf16[2,528,128]{2,1,0:T(8,128)(2,1)}, bf16[2,528,128]{2,1,0:T(8,128)(2,1)S(1)}, u32[]{:S(2)}, u32[]{:S(2)}) collective-permute-start(bf16[2,528,128]{2,1,0:T(8,128)(2,1)} %collective-permute-done.3.refs_2_.refs_15_), channel_id=1, source_target_pairs={{0,16},{16,0},{32,48},{48,32},{64,80},{80,64},{96,112},{112,96},{1... | collective-permute-start | bytes 811016 | tf_op jit(solution)/shard_map/ppermute | solution.py:475
  35.2 6.3 %collective-permute-start.18 = (bf16[2,512,128]{2,1,0:T(8,128)(2,1)}, bf16[2,512,128]{2,1,0:T(8,128)(2,1)}, u32[]{:S(2)}, u32[]{:S(2)}) collective-permute-start(bf16[2,512,128]{2,1,0:T(8,128)(2,1)} %collective-permute-done.16.refs_21_), channel_id=1, source_target_pairs={{0,32},{32,64},{64,96},{96,128},{128,160},{160,192},{192,224},{224... | collective-permute-start | bytes 786440 | tf_op jit(solution)/shard_map/ppermute | solution.py:478
  37.8 1.7 %collective-permute-start.9 = (bf16[2,128,256]{2,1,0:T(8,128)(2,1)S(1)}, bf16[2,128,256]{2,1,0:T(8,128)(2,1)S(1)}, u32[]{:S(2)}, u32[]{:S(2)}) collective-permute-start(bf16[2,128,256]{2,1,0:T(8,128)(2,1)S(1)} %collective-permute-done.8.refs_7_), channel_id=1, source_target_pairs={{0,16},{16,0},{32,48},{48,32},{64,80},{80,64},{96,112},{112,96},{1... | collective-permute-start | bytes 393224 | tf_op jit(solution)/shard_map/ppermute | solution.py:475
  38.5 0.6 copy-start.16
  39.5 0.6 copy-start.18
  40.2 18.7 %collective-permute-start.12 = (bf16[2,528,128]{2,1,0:T(8,128)(2,1)}, bf16[2,528,128]{2,1,0:T(8,128)(2,1)}, u32[]{:S(2)}, u32[]{:S(2)}) collective-permute-start(bf16[2,528,128]{2,1,0:T(8,128)(2,1)} %collective-permute-done.3.refs_2_.refs_15_), channel_id=1, source_target_pairs={{0,32},{32,64},{64,96},{96,128},{128,160},{160,192},{192,224},{224... | collective-permute-start | bytes 811016 | tf_op jit(solution)/shard_map/ppermute | solution.py:478
  40.2 0.7 copy-start.2
  40.9 20.2 %collective-permute-start.15 = (bf16[2,512,128]{2,1,0:T(8,128)(2,1)}, bf16[2,512,128]{2,1,0:T(8,128)(2,1)}, u32[]{:S(2)}, u32[]{:S(2)}) collective-permute-start(bf16[2,512,128]{2,1,0:T(8,128)(2,1)} %collective-permute-done.14.refs_19_), channel_id=1, source_target_pairs={{0,16},{16,0},{32,48},{48,32},{64,80},{80,64},{96,112},{112,96},{1... | collective-permute-start | bytes 786440 | tf_op jit(solution)/shard_map/ppermute | solution.py:475
  41.5 19.6 %collective-permute-start.17 = (bf16[2,512,128]{2,1,0:T(8,128)(2,1)}, bf16[2,512,128]{2,1,0:T(8,128)(2,1)}, u32[]{:S(2)}, u32[]{:S(2)}) collective-permute-start(bf16[2,512,128]{2,1,0:T(8,128)(2,1)} %collective-permute-done.16.refs_21_), channel_id=1, source_target_pairs={{0,16},{16,0},{32,48},{48,32},{64,80},{80,64},{96,112},{112,96},{1... | collective-permute-start | bytes 786440 | tf_op jit(solution)/shard_map/ppermute | solution.py:475
  43.5 0.7 copy-start.4
  44.2 16.9 %collective-permute-start.19 = (bf16[2,512,128]{2,1,0:T(8,128)(2,1)}, bf16[2,512,128]{2,1,0:T(8,128)(2,1)}, u32[]{:S(2)}, u32[]{:S(2)}) collective-permute-start(bf16[2,512,128]{2,1,0:T(8,128)(2,1)} %collective-permute-done.18.refs_23_), channel_id=1, source_target_pairs={{0,16},{16,0},{32,48},{48,32},{64,80},{80,64},{96,112},{112,96},{1... | collective-permute-start | bytes 786440 | tf_op jit(solution)/shard_map/ppermute | solution.py:475
  44.2 0.7 copy-start.6
  44.9 16.2 %collective-permute-start.20 = (bf16[2,512,128]{2,1,0:T(8,128)(2,1)}, bf16[2,512,128]{2,1,0:T(8,128)(2,1)}, u32[]{:S(2)}, u32[]{:S(2)}) collective-permute-start(bf16[2,512,128]{2,1,0:T(8,128)(2,1)} %collective-permute-done.18.refs_23_), channel_id=1, source_target_pairs={{0,32},{32,64},{64,96},{96,128},{128,160},{160,192},{192,224},{224... | collective-permute-start | bytes 786440 | tf_op jit(solution)/shard_map/ppermute | solution.py:478
  46.5 0.9 %copy-start.20 = (bf16[128,640]{1,0:T(8,128)(2,1)S(1)}, bf16[128,640]{1,0:T(8,128)(2,1)}, u32[]{:S(2)}) copy-start(bf16[128,640]{1,0:T(8,128)(2,1)} %refs_1_.1) | copy-start | bytes 491524
  47.4 0.9 %copy-start.21 = (bf16[128,640]{1,0:T(8,128)(2,1)S(1)}, bf16[128,640]{1,0:T(8,128)(2,1)}, u32[]{:S(2)}) copy-start(bf16[128,640]{1,0:T(8,128)(2,1)} %refs_2_.1) | copy-start | bytes 491524
  49.5 1.0 %copy-start.3 = (bf16[2,528,128]{2,1,0:T(8,128)(2,1)S(1)}, bf16[2,528,128]{2,1,0:T(8,128)(2,1)}, u32[]{:S(2)}) copy-start(bf16[2,528,128]{2,1,0:T(8,128)(2,1)} %copy-done.2) | copy-start | bytes 811012
  50.5 2.2 %copy-start.1 = (bf16[2,528,128]{2,1,0:T(8,128)(2,1)S(1)}, bf16[2,528,128]{2,1,0:T(8,128)(2,1)}, u32[]{:S(2)}) copy-start(bf16[2,528,128]{2,1,0:T(8,128)(2,1)} %copy-done) | copy-start | bytes 811012
  50.5 2.2 %copy-start.5 = (bf16[2,528,128]{2,1,0:T(8,128)(2,1)S(1)}, bf16[2,528,128]{2,1,0:T(8,128)(2,1)}, u32[]{:S(2)}) copy-start(bf16[2,528,128]{2,1,0:T(8,128)(2,1)} %copy-done.4) | copy-start | bytes 811012
  52.7 2.3 %copy-start.7 = (bf16[2,528,128]{2,1,0:T(8,128)(2,1)S(1)}, bf16[2,528,128]{2,1,0:T(8,128)(2,1)}, u32[]{:S(2)}) copy-start(bf16[2,528,128]{2,1,0:T(8,128)(2,1)} %copy-done.6) | copy-start | bytes 811012
  52.7 2.3 %copy-start.11 = (bf16[2,128,256]{2,1,0:T(8,128)(2,1)S(1)}, bf16[2,128,256]{2,1,0:T(8,128)(2,1)}, u32[]{:S(2)}) copy-start(bf16[2,128,256]{2,1,0:T(8,128)(2,1)} %copy-done.10) | copy-start | bytes 393220
  52.7 2.3 %copy-start.13 = (bf16[2,128,256]{2,1,0:T(8,128)(2,1)S(1)}, bf16[2,128,256]{2,1,0:T(8,128)(2,1)}, u32[]{:S(2)}) copy-start(bf16[2,128,256]{2,1,0:T(8,128)(2,1)} %copy-done.12) | copy-start | bytes 393220
  52.7 2.3 %copy-start.15 = (bf16[2,128,256]{2,1,0:T(8,128)(2,1)S(1)}, bf16[2,128,256]{2,1,0:T(8,128)(2,1)}, u32[]{:S(2)}) copy-start(bf16[2,128,256]{2,1,0:T(8,128)(2,1)} %copy-done.14) | copy-start | bytes 393220
  52.8 2.3 %copy-start.17 = (bf16[2,128,256]{2,1,0:T(8,128)(2,1)S(1)}, bf16[2,128,256]{2,1,0:T(8,128)(2,1)}, u32[]{:S(2)}) copy-start(bf16[2,128,256]{2,1,0:T(8,128)(2,1)} %copy-done.16) | copy-start | bytes 393220
  52.8 2.3 %copy-start.19 = (bf16[2,128,256]{2,1,0:T(8,128)(2,1)S(1)}, bf16[2,128,256]{2,1,0:T(8,128)(2,1)}, u32[]{:S(2)}) copy-start(bf16[2,128,256]{2,1,0:T(8,128)(2,1)} %copy-done.18) | copy-start | bytes 393220
  58.9 2.2 %copy-start.9 = (bf16[2,512,128]{2,1,0:T(8,128)(2,1)S(1)}, bf16[2,512,128]{2,1,0:T(8,128)(2,1)}, u32[]{:S(2)}) copy-start(bf16[2,512,128]{2,1,0:T(8,128)(2,1)} %copy-done.8) | copy-start | bytes 786436
  70.1 1.5 %collective-permute-start.21 = (bf16[3,128,256]{2,1,0:T(8,128)(2,1)S(1)}, bf16[3,128,256]{2,1,0:T(8,128)(2,1)S(1)}, u32[]{:S(2)}, u32[]{:S(2)}) collective-permute-start(bf16[3,128,256]{2,1,0:T(8,128)(2,1)S(1)} %get-tuple-element.72), channel_id=1, source_target_pairs={{0,16},{16,0},{32,48},{48,32},{64,80},{80,64},{96,112},{112,96},{1... | collective-permute-start | bytes 589832 | tf_op jit(solution)/shard_map/ppermute | solution.py:475
  71.6 9.1 %collective-permute-start.22 = (bf16[2,128,256]{2,1,0:T(8,128)(2,1)S(1)}, bf16[2,128,256]{2,1,0:T(8,128)(2,1)S(1)}, u32[]{:S(2)}, u32[]{:S(2)}) collective-permute-start(bf16[2,128,256]{2,1,0:T(8,128)(2,1)S(1)} %merge.1), channel_id=1, source_target_pairs={{32,0},{64,32},{96,64},{128,96},{160,128},{192,160},{224,192},{80,... | collective-permute-start | bytes 393224 | tf_op jit(solution)/shard_map/ppermute | solution.py:511
  80.8 9.5 %collective-permute-start.23 = (bf16[2,128,256]{2,1,0:T(8,128)(2,1)S(1)}, bf16[2,128,256]{2,1,0:T(8,128)(2,1)S(1)}, u32[]{:S(2)}, u32[]{:S(2)}) collective-permute-start(bf16[2,128,256]{2,1,0:T(8,128)(2,1)S(1)} %collective-permute-done.22.near_ref), channel_id=1, source_target_pairs={{0,16},{16,0},{32,48},{48,32},{64,80},{80,64},{96,112},{112,96},{1... | collective-permute-start | bytes 393224 | tf_op jit(solution)/shard_map/ppermute | solution.py:475

commit v2 on v1

--- a/solution.py
+++ b/solution.py
@@ -453,8 +453,10 @@
 
     def finish():
         shared = (grads, state[2], factor, delta)
-        summed = grad_stage(*shared, partial, keys, values, rows, (0, tiles // 2), False)
-        return grad_stage(*shared, summed, keys, values, rows, (tiles // 2, tiles), True)
+        one, two = tiles // 4, tiles - tiles // 4
+        summed = grad_stage(*shared, partial, keys, values, rows, (0, one), False)
+        summed = grad_stage(*shared, summed, keys, values, rows, (one, two), False)
+        return grad_stage(*shared, summed, keys, values, rows, (two, tiles), True)
 
     return attended, finish, own, give, keep
 

time: 91.3 us -> 89.1 us (0.976)
  waiting for transfers between devices: 18 us -> 15.7 us
    ppermute x1, waiting for transfers between devices: 7.82 us -> 5.6 us  [local(): near = lax.ppermute(merge(keep, swapped), 'seq', back)]
    pallas_call x2 -> x3, Pallas kernels: 9.47 us -> 9.53 us  [grad_stage(): pl.pallas_call(functools.partial(grad_kernel, rows=rows, span=span, last=...]
  transfers between devices with their start and end apart: 24 -> 24, of which waited for: 9 -> 9; matrix products, arithmetic and copies ran while one was open for 2% -> 2% of each run, Pallas kernels for 23% -> 24%
where the time goes in v2:
time: 89.1 us; the launch traced here: 88.7 us
  Pallas kernels  30.7 us (34%)
  starting transfers between devices  29.1 us (33%)
  waiting for transfers between devices  15.7 us (18%)
  local copies, waits for them, and re-layouts  8.85 us (10%)
  other arithmetic  3.38 us (4%)
  between operations  0.98 us (1%)
    ppermute x10, starting transfers between devices, turn(): return lax.ppermute(block, 'seq', ring)  16.7 us
    pallas_call x5, Pallas kernels, stats(): pl.pallas_call(functools.partial(stats_kernel, rows=rows, tile=tile, star...  11.5 us
    ppermute x13, starting transfers between devices, swap(): return lax.ppermute(block, 'seq', partner)  11 us
    pallas_call x3, Pallas kernels, grad_stage(): pl.pallas_call(functools.partial(grad_kernel, rows=rows, span=span, last=...  9.53 us
    pallas_call x1, Pallas kernels, value_stage(): pl.pallas_call(functools.partial(value_kernel, rows=rows, tile=tile, coun...  8.97 us
    unnamed x44, local copies, waits for them, and re-layouts  8.85 us
    ppermute x10, waiting for transfers between devices, turn(): return lax.ppermute(block, 'seq', ring)  7.03 us
    ppermute x1, waiting for transfers between devices, local(): near = lax.ppermute(merge(keep, swapped), 'seq', back)  5.6 us
  transfers between devices with their start and end apart: 24, of which 9 were waited for; matrix products, arithmetic and copies ran while one was open for 2% of the time, Pallas kernels for 24%

profile of v2, /device:TPU:1, one launch (start us, length us, event | category | flops | bytes accessed | tf_op | source)
XLA Modules:
  0.0 88.7 jit_solution(900884981949923976)
XLA Ops:
  0.6 0.7 fusion.7
  1.3 0.9 %maximum_bitcast_fusion = bf16[1,528,128]{2,1,0:T(8,128)(2,1)S(1)} fusion(bf16[16,128]{1,0:T(8,128)(2,1)S(1)} %fusion.2, bf16[512,128]{1,0:T(8,128)(2,1)} %param.10), kind=kLoop, calls=%fused_computation.2 | loop fusion | flops 270336 | bytes 270336 | tf_op jit(solution)/shard_map/broadcast_in_dim | solution.py:485
  2.3 3.3 %collective-permute-start = (bf16[1,528,128]{2,1,0:T(8,128)(2,1)S(1)}, bf16[1,528,128]{2,1,0:T(8,128)(2,1)S(1)}, u32[]{:S(2)}, u32[]{:S(2)}) collective-permute-start(bf16[1,528,128]{2,1,0:T(8,128)(2,1)S(1)} %maximum_bitcast_fusion), channel_id=1, source_target_pairs={{0,16},{16,0},{32,48},{48,32},{64,80},{80,64},{96,112},{112,96},{1... | collective-permute-start | bytes 405512 | tf_op jit(solution)/shard_map/ppermute | solution.py:477
  5.5 1.0 %collective-permute-done = bf16[1,528,128]{2,1,0:T(8,128)(2,1)S(1)} collective-permute-done((bf16[1,528,128]{2,1,0:T(8,128)(2,1)S(1)}, bf16[1,528,128]{2,1,0:T(8,128)(2,1)S(1)}, u32[]{:S(2)}, u32[]{:S(2)}) %collective-permute-start) | collective-permute-done | bytes 135200 | tf_op jit(solution)/shard_map/ppermute | solution.py:477
  6.6 3.9 %collective-permute-start.1 = (bf16[2,528,128]{2,1,0:T(8,128)(2,1)S(1)}, bf16[2,528,128]{2,1,0:T(8,128)(2,1)S(1)}, u32[]{:S(2)}, u32[]{:S(2)}) collective-permute-start(bf16[2,528,128]{2,1,0:T(8,128)(2,1)S(1)} %pad_maximum_fusion.refs_3_.refs_10_), channel_id=1, source_target_pairs={{0,32},{32,64},{64,96},{96,128},{128,160},{160,192},{192,224},{224... | collective-permute-start | bytes 811016 | tf_op jit(solution)/shard_map/ppermute | solution.py:480
  10.5 3.4 %collective-permute-done.1.refs_2_.refs_11_ = bf16[2,528,128]{2,1,0:T(8,128)(2,1)S(1)} collective-permute-done((bf16[2,528,128]{2,1,0:T(8,128)(2,1)S(1)}, bf16[2,528,128]{2,1,0:T(8,128)(2,1)S(1)}, u32[]{:S(2)}, u32[]{:S(2)}) %collective-permute-start.1) | collective-permute-done | bytes 270368 | tf_op jit(solution)/shard_map/ppermute | solution.py:480
  13.9 3.1 %collective-permute-start.2 = (bf16[2,528,128]{2,1,0:T(8,128)(2,1)S(1)}, bf16[2,528,128]{2,1,0:T(8,128)(2,1)S(1)}, u32[]{:S(2)}, u32[]{:S(2)}) collective-permute-start(bf16[2,528,128]{2,1,0:T(8,128)(2,1)S(1)} %collective-permute-done.1.refs_2_.refs_11_), channel_id=1, source_target_pairs={{0,32},{32,64},{64,96},{96,128},{128,160},{160,192},{192,224},{224... | collective-permute-start | bytes 811016 | tf_op jit(solution)/shard_map/ppermute | solution.py:480
  17.0 0.9 %pad_maximum_fusion.1.refs_18_ = bf16[2,512,128]{2,1,0:T(8,128)(2,1)S(1)} fusion(bf16[1,512,128]{2,1,0:T(8,128)(2,1)S(1)} %collective-permute-done.13, bf16[1,512,128]{2,1,0:T(8,128)(2,1)} %bitcast.11), kind=kLoop, calls=%fused_computation.1 | loop fusion | flops 131072 | bytes 524288 | tf_op jit(solution)/shard_map/concatenate | solution.py:489
  18.1 0.8 maximum_bitcast_fusion.1
  19.0 1.5 %collective-permute-done.2.refs_2_.refs_13_ = bf16[2,528,128]{2,1,0:T(8,128)(2,1)S(1)} collective-permute-done((bf16[2,528,128]{2,1,0:T(8,128)(2,1)S(1)}, bf16[2,528,128]{2,1,0:T(8,128)(2,1)S(1)}, u32[]{:S(2)}, u32[]{:S(2)}) %collective-permute-start.2) | collective-permute-done | bytes 270368 | tf_op jit(solution)/shard_map/ppermute | solution.py:480
  20.4 3.1 %collective-permute-start.3 = (bf16[2,528,128]{2,1,0:T(8,128)(2,1)S(1)}, bf16[2,528,128]{2,1,0:T(8,128)(2,1)}, u32[]{:S(2)}, u32[]{:S(2)}) collective-permute-start(bf16[2,528,128]{2,1,0:T(8,128)(2,1)S(1)} %collective-permute-done.2.refs_2_.refs_13_), channel_id=1, source_target_pairs={{0,32},{32,64},{64,96},{96,128},{128,160},{160,192},{192,224},{224... | collective-permute-start | bytes 811016 | tf_op jit(solution)/shard_map/ppermute | solution.py:480
  23.7 0.6 copy-done.10
  24.3 2.1 %collective-permute-start.16 = (bf16[2,512,128]{2,1,0:T(8,128)(2,1)}, bf16[2,512,128]{2,1,0:T(8,128)(2,1)}, u32[]{:S(2)}, u32[]{:S(2)}) collective-permute-start(bf16[2,512,128]{2,1,0:T(8,128)(2,1)} %collective-permute-done.14.refs_19_), channel_id=1, source_target_pairs={{0,32},{32,64},{64,96},{96,128},{128,160},{160,192},{192,224},{224... | collective-permute-start | bytes 786440 | tf_op jit(solution)/shard_map/ppermute | solution.py:480
  26.5 1.9 %collective-permute-done.6.refs_5_ = bf16[2,128,256]{2,1,0:T(8,128)(2,1)S(1)} collective-permute-done((bf16[2,128,256]{2,1,0:T(8,128)(2,1)S(1)}, bf16[2,128,256]{2,1,0:T(8,128)(2,1)S(1)}, u32[]{:S(2)}, u32[]{:S(2)}) %collective-permute-start.6) | collective-permute-done | bytes 131104 | tf_op jit(solution)/shard_map/ppermute | solution.py:480
  28.4 4.0 %collective-permute-start.7 = (bf16[2,128,256]{2,1,0:T(8,128)(2,1)S(1)}, bf16[2,128,256]{2,1,0:T(8,128)(2,1)S(1)}, u32[]{:S(2)}, u32[]{:S(2)}) collective-permute-start(bf16[2,128,256]{2,1,0:T(8,128)(2,1)S(1)} %collective-permute-done.6.refs_5_), channel_id=1, source_target_pairs={{0,16},{16,0},{32,48},{48,32},{64,80},{80,64},{96,112},{112,96},{1... | collective-permute-start | bytes 393224 | tf_op jit(solution)/shard_map/ppermute | solution.py:477
  32.3 0.7 copy-done.12
  33.0 0.3 collective-permute-done.7.refs_6_
  33.3 0.7 copy-done.14
  34.0 0.4 collective-permute-start.10
  34.3 0.7 copy-done
  35.2 2.6 %collective-permute-start.18 = (bf16[2,512,128]{2,1,0:T(8,128)(2,1)}, bf16[2,512,128]{2,1,0:T(8,128)(2,1)}, u32[]{:S(2)}, u32[]{:S(2)}) collective-permute-start(bf16[2,512,128]{2,1,0:T(8,128)(2,1)} %collective-permute-done.16.refs_21_), channel_id=1, source_target_pairs={{0,32},{32,64},{64,96},{96,128},{128,160},{160,192},{192,224},{224... | collective-permute-start | bytes 786440 | tf_op jit(solution)/shard_map/ppermute | solution.py:480
  37.8 0.7 collective-permute-start.9
  38.5 0.6 copy-done.16
  39.2 0.3 collective-permute-done.9.refs_8_
  39.5 0.6 copy-done.18
  40.2 0.7 copy-done.2
  40.9 0.4 collective-permute-start.15
  41.2 0.2 collective-permute-done.18.refs_23_
  41.5 2.0 %collective-permute-start.17 = (bf16[2,512,128]{2,1,0:T(8,128)(2,1)}, bf16[2,512,128]{2,1,0:T(8,128)(2,1)}, u32[]{:S(2)}, u32[]{:S(2)}) collective-permute-start(bf16[2,512,128]{2,1,0:T(8,128)(2,1)} %collective-permute-done.16.refs_21_), channel_id=1, source_target_pairs={{0,16},{16,0},{32,48},{48,32},{64,80},{80,64},{96,112},{112,96},{1... | collective-permute-start | bytes 786440 | tf_op jit(solution)/shard_map/ppermute | solution.py:477
  43.5 0.7 copy-done.4
  44.2 0.7 copy-done.6
  44.9 1.6 %collective-permute-start.20 = (bf16[2,512,128]{2,1,0:T(8,128)(2,1)}, bf16[2,512,128]{2,1,0:T(8,128)(2,1)}, u32[]{:S(2)}, u32[]{:S(2)}) collective-permute-start(bf16[2,512,128]{2,1,0:T(8,128)(2,1)} %collective-permute-done.18.refs_23_), channel_id=1, source_target_pairs={{0,32},{32,64},{64,96},{96,128},{128,160},{160,192},{192,224},{224... | collective-permute-start | bytes 786440 | tf_op jit(solution)/shard_map/ppermute | solution.py:480
  46.5 0.9 %copy-done.20 = bf16[128,640]{1,0:T(8,128)(2,1)S(1)} copy-done((bf16[128,640]{1,0:T(8,128)(2,1)S(1)}, bf16[128,640]{1,0:T(8,128)(2,1)}, u32[]{:S(2)}) %copy-start.20) | copy-done | bytes 163864
  47.4 0.9 %copy-done.21 = bf16[128,640]{1,0:T(8,128)(2,1)S(1)} copy-done((bf16[128,640]{1,0:T(8,128)(2,1)S(1)}, bf16[128,640]{1,0:T(8,128)(2,1)}, u32[]{:S(2)}) %copy-start.21) | copy-done | bytes 163864
  48.3 1.2 %stats.5 = (f32[640,128]{1,0:T(8,128)S(1)}, f32[640,128]{1,0:T(8,128)S(1)}, f32[16,640,512]{2,1,0:T(8,128)S(1)}, f32[16,640,128]{2,1,0:T(8,128)S(1)}, bf16[640,1...) custom-call(s32[1]{0:T(128)} %bitcast.refs_0_.meta_ref, bf16[128,640]{1,0:T(8,128)(2,1)S(1)} %copy-done.20, ...), custom_call_target="tpu_custom_call" | custom-call | flops 167772160 | bytes 262144 | tf_op jit(solution)/shard_map/stats/pallas_call | solution.py:192
  49.5 0.9 %copy-done.3 = bf16[2,528,128]{2,1,0:T(8,128)(2,1)S(1)} copy-done((bf16[2,528,128]{2,1,0:T(8,128)(2,1)S(1)}, bf16[2,528,128]{2,1,0:T(8,128)(2,1)}, u32[]{:S(2)}) %copy-start.3) | copy-done | bytes 270360
  50.5 2.2 %stats.6 = (f32[640,128]{1,0:T(8,128)S(1)}, f32[640,128]{1,0:T(8,128)S(1)}, f32[16,640,512]{2,1,0:T(8,128)S(1)}, f32[16,640,128]{2,1,0:T(8,128)S(1)}) custom-call(s32[1]{0:T(128)} %bitcast.refs_0_.meta_ref, bf16[640,128]{1,0:T(8,128)(2,1)S(1)} %get-tuple-element.40.refs_1_, ...), custom_call_target="tpu_custom_call", output_to_operand_aliasing={{2}: (6, {}), {3}: (7, {})} | custom-call | flops 335544320 | bytes 524288 | tf_op jit(solution)/shard_map/stats/pallas_call | solution.py:192
  52.8 2.2 %stats.7 = (f32[640,128]{1,0:T(8,128)S(1)}, f32[640,128]{1,0:T(8,128)S(1)}, f32[16,640,512]{2,1,0:T(8,128)S(1)}, f32[16,640,128]{2,1,0:T(8,128)S(1)}) custom-call(s32[1]{0:T(128)} %bitcast.refs_0_.meta_ref, bf16[640,128]{1,0:T(8,128)(2,1)S(1)} %get-tuple-element.40.refs_1_, ...), custom_call_target="tpu_custom_call", output_to_operand_aliasing={{2}: (6, {}), {3}: (7, {})} | custom-call | flops 335544320 | bytes 524288 | tf_op jit(solution)/shard_map/stats/pallas_call | solution.py:192
  55.0 3.8 %stats.8 = (f32[640,128]{1,0:T(8,128)S(1)}, f32[640,128]{1,0:T(8,128)S(1)}, f32[16,640,512]{2,1,0:T(8,128)S(1)}, f32[16,640,128]{2,1,0:T(8,128)S(1)}, f32[640,64...) custom-call(s32[1]{0:T(128)} %bitcast.refs_0_.meta_ref, ...), custom_call_target="tpu_custom_call", output_to_operand_aliasing={{2}: (11, {}), {3}: (12, {})} | custom-call | flops 335544320 | bytes 524288 | tf_op jit(solution)/shard_map/stats/pallas_call | solution.py:192
  58.9 2.1 %stats.9 = (f32[640,128]{1,0:T(8,128)S(1)}, f32[640,128]{1,0:T(8,128)S(1)}, f32[16,640,512]{2,1,0:T(8,128)S(1)}, f32[16,640,128]{2,1,0:T(8,128)S(1)}) custom-call(s32[1]{0:T(128)} %bitcast.refs_0_.meta_ref, bf16[640,128]{1,0:T(8,128)(2,1)S(1)} %get-tuple-element.40.refs_1_, ...), custom_call_target="tpu_custom_call", output_to_operand_aliasing={{2}: (5, {}), {3}: (6, {})} | custom-call | flops 167772160 | bytes 262144 | tf_op jit(solution)/shard_map/stats/pallas_call | solution.py:192
  61.1 9.0 %value_stage.1 = (bf16[128,640]{1,0:T(8,128)(2,1)}, f32[16,640,128]{2,1,0:T(8,128)S(1)}, f32[640,128]{1,0:T(8,128)S(1)}, f32[640,128]{1,0:T(8,128)S(1)}, bf16[16...) custom-call(s32[1]{0:T(128)} %bitcast.refs_0_.meta_ref, ...), custom_call_target="tpu_custom_call", output_to_operand_aliasing={{1}: (7, {})} | custom-call | flops 1342177280 | bytes 1048576 | tf_op jit(solution)/shard_map/value_stage/pallas_call | solution.py:360
  70.2 1.4 %collective-permute-done.21.swapped_ref = bf16[3,128,256]{2,1,0:T(8,128)(2,1)S(1)} collective-permute-done((bf16[3,128,256]{2,1,0:T(8,128)(2,1)S(1)}, bf16[3,128,256]{2,1,0:T(8,128)(2,1)S(1)}, u32[]{:S(2)}, u32[]{:S(2)}) %collective-permute-start.21) | collective-permute-done | bytes 196640 | tf_op jit(solution)/shard_map/ppermute | solution.py:477
  71.6 1.3 %collective-permute-start.22 = (bf16[2,128,256]{2,1,0:T(8,128)(2,1)S(1)}, bf16[2,128,256]{2,1,0:T(8,128)(2,1)S(1)}, u32[]{:S(2)}, u32[]{:S(2)}) collective-permute-start(bf16[2,128,256]{2,1,0:T(8,128)(2,1)S(1)} %merge.1), channel_id=1, source_target_pairs={{32,0},{64,32},{96,64},{128,96},{160,128},{192,160},{224,192},{80,... | collective-permute-start | bytes 393224 | tf_op jit(solution)/shard_map/ppermute | solution.py:513
  72.9 2.2 %grad_stage.3.partial_ref = f32[640,128]{1,0:T(8,128)S(1)} custom-call(bf16[640,128]{1,0:T(8,128)(2,1)S(1)} %get-tuple-element.41.refs_2_.grads, f32[16,640,512]{2,1,0:T(8,128)S(1)} %get-tuple-element.61.refs_6_.raised, f32[16,640,128]{2,1,0:T(8,128)S(1)} %get-tuple-element.66.factor_ref, f32[640,128]{1,0:T(8,128)S(1)} %get-tuple-element.67.delta, ...), custom_call_target="tpu_custom_call" | custom-call | flops 671088640 | bytes 1048576 | tf_op jit(solution)/shard_map/grad_stage/pallas_call | solution.py:395
  75.1 5.6 %collective-permute-done.22.near_ref = bf16[2,128,256]{2,1,0:T(8,128)(2,1)S(1)} collective-permute-done((bf16[2,128,256]{2,1,0:T(8,128)(2,1)S(1)}, bf16[2,128,256]{2,1,0:T(8,128)(2,1)S(1)}, u32[]{:S(2)}, u32[]{:S(2)}) %collective-permute-start.22) | collective-permute-done | bytes 131104 | tf_op jit(solution)/shard_map/ppermute | solution.py:513
  80.8 4.4 %grad_stage.4.partial_ref = f32[640,128]{1,0:T(8,128)S(1)} custom-call(bf16[640,128]{1,0:T(8,128)(2,1)S(1)} %get-tuple-element.41.refs_2_.grads, f32[16,640,512]{2,1,0:T(8,128)S(1)} %get-tuple-element.61.refs_6_.raised, f32[16,640,128]{2,1,0:T(8,128)S(1)} %get-tuple-element.66.factor_ref, f32[640,128]{1,0:T(8,128)S(1)} %get-tuple-element.67.delta, ...), custom_call_target="tpu_custom_call" | custom-call | flops 1342177280 | bytes 1048576 | tf_op jit(solution)/shard_map/grad_stage/pallas_call | solution.py:395
  85.2 2.9 %grad_stage.5 = bf16[128,640]{1,0:T(8,128)(2,1)} custom-call(bf16[640,128]{1,0:T(8,128)(2,1)S(1)} %get-tuple-element.41.refs_2_.grads, f32[16,640,512]{2,1,0:T(8,128)S(1)} %get-tuple-element.61.refs_6_.raised, f32[16,640,128]{2,1,0:T(8,128)S(1)} %get-tuple-element.66.factor_ref, f32[640,128]{1,0:T(8,128)S(1)} %get-tuple-element.67.delta, ...), custom_call_target="tpu_custom_call" | custom-call | flops 671088640 | bytes 1048576 | tf_op jit(solution)/shard_map/grad_stage/pallas_call | solution.py:395
  88.1 0.7 combine.1
  (62 shorter events, 0.7 us)
Async XLA Ops:
  2.3 4.3 %collective-permute-start = (bf16[1,528,128]{2,1,0:T(8,128)(2,1)S(1)}, bf16[1,528,128]{2,1,0:T(8,128)(2,1)S(1)}, u32[]{:S(2)}, u32[]{:S(2)}) collective-permute-start(bf16[1,528,128]{2,1,0:T(8,128)(2,1)S(1)} %maximum_bitcast_fusion), channel_id=1, source_target_pairs={{0,16},{16,0},{32,48},{48,32},{64,80},{80,64},{96,112},{112,96},{1... | collective-permute-start | bytes 405512 | tf_op jit(solution)/shard_map/ppermute | solution.py:477
  6.6 7.3 %collective-permute-start.1 = (bf16[2,528,128]{2,1,0:T(8,128)(2,1)S(1)}, bf16[2,528,128]{2,1,0:T(8,128)(2,1)S(1)}, u32[]{:S(2)}, u32[]{:S(2)}) collective-permute-start(bf16[2,528,128]{2,1,0:T(8,128)(2,1)S(1)} %pad_maximum_fusion.refs_3_.refs_10_), channel_id=1, source_target_pairs={{0,32},{32,64},{64,96},{96,128},{128,160},{160,192},{192,224},{224... | collective-permute-start | bytes 811016 | tf_op jit(solution)/shard_map/ppermute | solution.py:480
  10.5 6.5 %collective-permute-start.13 = (bf16[1,512,128]{2,1,0:T(8,128)(2,1)}, bf16[1,512,128]{2,1,0:T(8,128)(2,1)S(1)}, u32[]{:S(2)}, u32[]{:S(2)}) collective-permute-start(bf16[1,512,128]{2,1,0:T(8,128)(2,1)} %bitcast.10), channel_id=1, source_target_pairs={{0,16},{16,0},{32,48},{48,32},{64,80},{80,64},{96,112},{112,96},{1... | collective-permute-start | bytes 393224 | tf_op jit(solution)/shard_map/ppermute | solution.py:477
  13.9 6.5 %collective-permute-start.2 = (bf16[2,528,128]{2,1,0:T(8,128)(2,1)S(1)}, bf16[2,528,128]{2,1,0:T(8,128)(2,1)S(1)}, u32[]{:S(2)}, u32[]{:S(2)}) collective-permute-start(bf16[2,528,128]{2,1,0:T(8,128)(2,1)S(1)} %collective-permute-done.1.refs_2_.refs_11_), channel_id=1, source_target_pairs={{0,32},{32,64},{64,96},{96,128},{128,160},{160,192},{192,224},{224... | collective-permute-start | bytes 811016 | tf_op jit(solution)/shard_map/ppermute | solution.py:480
  18.0 26.2 %copy-start.8 = (bf16[2,512,128]{2,1,0:T(8,128)(2,1)}, bf16[2,512,128]{2,1,0:T(8,128)(2,1)S(1)}, u32[]{:S(2)}) copy-start(bf16[2,512,128]{2,1,0:T(8,128)(2,1)S(1)} %pad_maximum_fusion.1.refs_18_) | copy-start | bytes 786436
  18.0 6.3 %collective-permute-start.14 = (bf16[2,512,128]{2,1,0:T(8,128)(2,1)S(1)}, bf16[2,512,128]{2,1,0:T(8,128)(2,1)}, u32[]{:S(2)}, u32[]{:S(2)}) collective-permute-start(bf16[2,512,128]{2,1,0:T(8,128)(2,1)S(1)} %pad_maximum_fusion.1.refs_18_), channel_id=1, source_target_pairs={{0,32},{32,64},{64,96},{96,128},{128,160},{160,192},{192,224},{224... | collective-permute-start | bytes 786440 | tf_op jit(solution)/shard_map/ppermute | solution.py:480
  18.9 4.7 %collective-permute-start.5 = (bf16[1,128,256]{2,1,0:T(8,128)(2,1)S(1)}, bf16[1,128,256]{2,1,0:T(8,128)(2,1)S(1)}, u32[]{:S(2)}, u32[]{:S(2)}) collective-permute-start(bf16[1,128,256]{2,1,0:T(8,128)(2,1)S(1)} %maximum_bitcast_fusion.1), channel_id=1, source_target_pairs={{0,16},{16,0},{32,48},{48,32},{64,80},{80,64},{96,112},{112,96},{1... | collective-permute-start | bytes 196616 | tf_op jit(solution)/shard_map/ppermute | solution.py:477
  20.4 14.6 %collective-permute-start.3 = (bf16[2,528,128]{2,1,0:T(8,128)(2,1)S(1)}, bf16[2,528,128]{2,1,0:T(8,128)(2,1)}, u32[]{:S(2)}, u32[]{:S(2)}) collective-permute-start(bf16[2,528,128]{2,1,0:T(8,128)(2,1)S(1)} %collective-permute-done.2.refs_2_.refs_13_), channel_id=1, source_target_pairs={{0,32},{32,64},{64,96},{96,128},{128,160},{160,192},{192,224},{224... | collective-permute-start | bytes 811016 | tf_op jit(solution)/shard_map/ppermute | solution.py:480
  23.6 4.8 %collective-permute-start.6 = (bf16[2,128,256]{2,1,0:T(8,128)(2,1)S(1)}, bf16[2,128,256]{2,1,0:T(8,128)(2,1)S(1)}, u32[]{:S(2)}, u32[]{:S(2)}) collective-permute-start(bf16[2,128,256]{2,1,0:T(8,128)(2,1)S(1)} %pad_maximum_fusion.2.refs_4_), channel_id=1, source_target_pairs={{0,32},{32,64},{64,96},{96,128},{128,160},{160,192},{192,224},{224... | collective-permute-start | bytes 393224 | tf_op jit(solution)/shard_map/ppermute | solution.py:480
  23.7 0.7 copy-start.10
  24.3 10.9 %collective-permute-start.16 = (bf16[2,512,128]{2,1,0:T(8,128)(2,1)}, bf16[2,512,128]{2,1,0:T(8,128)(2,1)}, u32[]{:S(2)}, u32[]{:S(2)}) collective-permute-start(bf16[2,512,128]{2,1,0:T(8,128)(2,1)} %collective-permute-done.14.refs_19_), channel_id=1, source_target_pairs={{0,32},{32,64},{64,96},{96,128},{128,160},{160,192},{192,224},{224... | collective-permute-start | bytes 786440 | tf_op jit(solution)/shard_map/ppermute | solution.py:480
  28.4 5.0 %collective-permute-start.7 = (bf16[2,128,256]{2,1,0:T(8,128)(2,1)S(1)}, bf16[2,128,256]{2,1,0:T(8,128)(2,1)S(1)}, u32[]{:S(2)}, u32[]{:S(2)}) collective-permute-start(bf16[2,128,256]{2,1,0:T(8,128)(2,1)S(1)} %collective-permute-done.6.refs_5_), channel_id=1, source_target_pairs={{0,16},{16,0},{32,48},{48,32},{64,80},{80,64},{96,112},{112,96},{1... | collective-permute-start | bytes 393224 | tf_op jit(solution)/shard_map/ppermute | solution.py:477
  32.3 5.5 %collective-permute-start.8 = (bf16[2,128,256]{2,1,0:T(8,128)(2,1)S(1)}, bf16[2,128,256]{2,1,0:T(8,128)(2,1)S(1)}, u32[]{:S(2)}, u32[]{:S(2)}) collective-permute-start(bf16[2,128,256]{2,1,0:T(8,128)(2,1)S(1)} %collective-permute-done.6.refs_5_), channel_id=1, source_target_pairs={{0,32},{32,64},{64,96},{96,128},{128,160},{160,192},{192,224},{224... | collective-permute-start | bytes 393224 | tf_op jit(solution)/shard_map/ppermute | solution.py:480
  32.3 0.7 copy-start.12
  33.0 7.2 %collective-permute-start.11 = (bf16[2,528,128]{2,1,0:T(8,128)(2,1)S(1)}, bf16[2,528,128]{2,1,0:T(8,128)(2,1)S(1)}, u32[]{:S(2)}, u32[]{:S(2)}) collective-permute-start(bf16[2,528,128]{2,1,0:T(8,128)(2,1)S(1)} %collective-permute-done.1.refs_2_.refs_11_), channel_id=1, source_target_pairs={{0,16},{16,0},{32,48},{48,32},{64,80},{80,64},{96,112},{112,96},{1... | collective-permute-start | bytes 811016 | tf_op jit(solution)/shard_map/ppermute | solution.py:477
  33.3 0.7 copy-start.14
  34.0 9.5 %collective-permute-start.10 = (bf16[2,528,128]{2,1,0:T(8,128)(2,1)S(1)}, bf16[2,528,128]{2,1,0:T(8,128)(2,1)S(1)}, u32[]{:S(2)}, u32[]{:S(2)}) collective-permute-start(bf16[2,528,128]{2,1,0:T(8,128)(2,1)S(1)} %collective-permute-done.2.refs_2_.refs_13_), channel_id=1, source_target_pairs={{0,16},{16,0},{32,48},{48,32},{64,80},{80,64},{96,112},{112,96},{1... | collective-permute-start | bytes 811016 | tf_op jit(solution)/shard_map/ppermute | solution.py:477
  34.3 0.7 copy-start
  35.0 9.1 %collective-permute-start.4 = (bf16[2,528,128]{2,1,0:T(8,128)(2,1)}, bf16[2,528,128]{2,1,0:T(8,128)(2,1)S(1)}, u32[]{:S(2)}, u32[]{:S(2)}) collective-permute-start(bf16[2,528,128]{2,1,0:T(8,128)(2,1)} %collective-permute-done.3.refs_2_.refs_15_), channel_id=1, source_target_pairs={{0,16},{16,0},{32,48},{48,32},{64,80},{80,64},{96,112},{112,96},{1... | collective-permute-start | bytes 811016 | tf_op jit(solution)/shard_map/ppermute | solution.py:477
  35.2 6.3 %collective-permute-start.18 = (bf16[2,512,128]{2,1,0:T(8,128)(2,1)}, bf16[2,512,128]{2,1,0:T(8,128)(2,1)}, u32[]{:S(2)}, u32[]{:S(2)}) collective-permute-start(bf16[2,512,128]{2,1,0:T(8,128)(2,1)} %collective-permute-done.16.refs_21_), channel_id=1, source_target_pairs={{0,32},{32,64},{64,96},{96,128},{128,160},{160,192},{192,224},{224... | collective-permute-start | bytes 786440 | tf_op jit(solution)/shard_map/ppermute | solution.py:480
  37.8 1.7 %collective-permute-start.9 = (bf16[2,128,256]{2,1,0:T(8,128)(2,1)S(1)}, bf16[2,128,256]{2,1,0:T(8,128)(2,1)S(1)}, u32[]{:S(2)}, u32[]{:S(2)}) collective-permute-start(bf16[2,128,256]{2,1,0:T(8,128)(2,1)S(1)} %collective-permute-done.8.refs_7_), channel_id=1, source_target_pairs={{0,16},{16,0},{32,48},{48,32},{64,80},{80,64},{96,112},{112,96},{1... | collective-permute-start | bytes 393224 | tf_op jit(solution)/shard_map/ppermute | solution.py:477
  38.5 0.6 copy-start.16
  39.5 0.6 copy-start.18
  40.2 18.7 %collective-permute-start.12 = (bf16[2,528,128]{2,1,0:T(8,128)(2,1)}, bf16[2,528,128]{2,1,0:T(8,128)(2,1)}, u32[]{:S(2)}, u32[]{:S(2)}) collective-permute-start(bf16[2,528,128]{2,1,0:T(8,128)(2,1)} %collective-permute-done.3.refs_2_.refs_15_), channel_id=1, source_target_pairs={{0,32},{32,64},{64,96},{96,128},{128,160},{160,192},{192,224},{224... | collective-permute-start | bytes 811016 | tf_op jit(solution)/shard_map/ppermute | solution.py:480
  40.2 0.7 copy-start.2
  40.9 20.2 %collective-permute-start.15 = (bf16[2,512,128]{2,1,0:T(8,128)(2,1)}, bf16[2,512,128]{2,1,0:T(8,128)(2,1)}, u32[]{:S(2)}, u32[]{:S(2)}) collective-permute-start(bf16[2,512,128]{2,1,0:T(8,128)(2,1)} %collective-permute-done.14.refs_19_), channel_id=1, source_target_pairs={{0,16},{16,0},{32,48},{48,32},{64,80},{80,64},{96,112},{112,96},{1... | collective-permute-start | bytes 786440 | tf_op jit(solution)/shard_map/ppermute | solution.py:477
  41.5 19.6 %collective-permute-start.17 = (bf16[2,512,128]{2,1,0:T(8,128)(2,1)}, bf16[2,512,128]{2,1,0:T(8,128)(2,1)}, u32[]{:S(2)}, u32[]{:S(2)}) collective-permute-start(bf16[2,512,128]{2,1,0:T(8,128)(2,1)} %collective-permute-done.16.refs_21_), channel_id=1, source_target_pairs={{0,16},{16,0},{32,48},{48,32},{64,80},{80,64},{96,112},{112,96},{1... | collective-permute-start | bytes 786440 | tf_op jit(solution)/shard_map/ppermute | solution.py:477
  43.5 0.7 copy-start.4
  44.2 16.9 %collective-permute-start.19 = (bf16[2,512,128]{2,1,0:T(8,128)(2,1)}, bf16[2,512,128]{2,1,0:T(8,128)(2,1)}, u32[]{:S(2)}, u32[]{:S(2)}) collective-permute-start(bf16[2,512,128]{2,1,0:T(8,128)(2,1)} %collective-permute-done.18.refs_23_), channel_id=1, source_target_pairs={{0,16},{16,0},{32,48},{48,32},{64,80},{80,64},{96,112},{112,96},{1... | collective-permute-start | bytes 786440 | tf_op jit(solution)/shard_map/ppermute | solution.py:477
  44.2 0.7 copy-start.6
  44.9 16.2 %collective-permute-start.20 = (bf16[2,512,128]{2,1,0:T(8,128)(2,1)}, bf16[2,512,128]{2,1,0:T(8,128)(2,1)}, u32[]{:S(2)}, u32[]{:S(2)}) collective-permute-start(bf16[2,512,128]{2,1,0:T(8,128)(2,1)} %collective-permute-done.18.refs_23_), channel_id=1, source_target_pairs={{0,32},{32,64},{64,96},{96,128},{128,160},{160,192},{192,224},{224... | collective-permute-start | bytes 786440 | tf_op jit(solution)/shard_map/ppermute | solution.py:480
  46.5 0.9 %copy-start.20 = (bf16[128,640]{1,0:T(8,128)(2,1)S(1)}, bf16[128,640]{1,0:T(8,128)(2,1)}, u32[]{:S(2)}) copy-start(bf16[128,640]{1,0:T(8,128)(2,1)} %refs_1_.1) | copy-start | bytes 491524
  47.4 0.9 %copy-start.21 = (bf16[128,640]{1,0:T(8,128)(2,1)S(1)}, bf16[128,640]{1,0:T(8,128)(2,1)}, u32[]{:S(2)}) copy-start(bf16[128,640]{1,0:T(8,128)(2,1)} %refs_2_.1) | copy-start | bytes 491524
  49.5 1.0 %copy-start.3 = (bf16[2,528,128]{2,1,0:T(8,128)(2,1)S(1)}, bf16[2,528,128]{2,1,0:T(8,128)(2,1)}, u32[]{:S(2)}) copy-start(bf16[2,528,128]{2,1,0:T(8,128)(2,1)} %copy-done.2) | copy-start | bytes 811012
  50.5 2.2 %copy-start.1 = (bf16[2,528,128]{2,1,0:T(8,128)(2,1)S(1)}, bf16[2,528,128]{2,1,0:T(8,128)(2,1)}, u32[]{:S(2)}) copy-start(bf16[2,528,128]{2,1,0:T(8,128)(2,1)} %copy-done) | copy-start | bytes 811012
  50.5 2.2 %copy-start.5 = (bf16[2,528,128]{2,1,0:T(8,128)(2,1)S(1)}, bf16[2,528,128]{2,1,0:T(8,128)(2,1)}, u32[]{:S(2)}) copy-start(bf16[2,528,128]{2,1,0:T(8,128)(2,1)} %copy-done.4) | copy-start | bytes 811012
  52.7 2.3 %copy-start.7 = (bf16[2,528,128]{2,1,0:T(8,128)(2,1)S(1)}, bf16[2,528,128]{2,1,0:T(8,128)(2,1)}, u32[]{:S(2)}) copy-start(bf16[2,528,128]{2,1,0:T(8,128)(2,1)} %copy-done.6) | copy-start | bytes 811012
  52.7 2.3 %copy-start.11 = (bf16[2,128,256]{2,1,0:T(8,128)(2,1)S(1)}, bf16[2,128,256]{2,1,0:T(8,128)(2,1)}, u32[]{:S(2)}) copy-start(bf16[2,128,256]{2,1,0:T(8,128)(2,1)} %copy-done.10) | copy-start | bytes 393220
  52.7 2.3 %copy-start.13 = (bf16[2,128,256]{2,1,0:T(8,128)(2,1)S(1)}, bf16[2,128,256]{2,1,0:T(8,128)(2,1)}, u32[]{:S(2)}) copy-start(bf16[2,128,256]{2,1,0:T(8,128)(2,1)} %copy-done.12) | copy-start | bytes 393220
  52.7 2.3 %copy-start.15 = (bf16[2,128,256]{2,1,0:T(8,128)(2,1)S(1)}, bf16[2,128,256]{2,1,0:T(8,128)(2,1)}, u32[]{:S(2)}) copy-start(bf16[2,128,256]{2,1,0:T(8,128)(2,1)} %copy-done.14) | copy-start | bytes 393220
  52.8 2.3 %copy-start.17 = (bf16[2,128,256]{2,1,0:T(8,128)(2,1)S(1)}, bf16[2,128,256]{2,1,0:T(8,128)(2,1)}, u32[]{:S(2)}) copy-start(bf16[2,128,256]{2,1,0:T(8,128)(2,1)} %copy-done.16) | copy-start | bytes 393220
  52.8 2.3 %copy-start.19 = (bf16[2,128,256]{2,1,0:T(8,128)(2,1)S(1)}, bf16[2,128,256]{2,1,0:T(8,128)(2,1)}, u32[]{:S(2)}) copy-start(bf16[2,128,256]{2,1,0:T(8,128)(2,1)} %copy-done.18) | copy-start | bytes 393220
  58.9 2.2 %copy-start.9 = (bf16[2,512,128]{2,1,0:T(8,128)(2,1)S(1)}, bf16[2,512,128]{2,1,0:T(8,128)(2,1)}, u32[]{:S(2)}) copy-start(bf16[2,512,128]{2,1,0:T(8,128)(2,1)} %copy-done.8) | copy-start | bytes 786436
  70.1 1.5 %collective-permute-start.21 = (bf16[3,128,256]{2,1,0:T(8,128)(2,1)S(1)}, bf16[3,128,256]{2,1,0:T(8,128)(2,1)S(1)}, u32[]{:S(2)}, u32[]{:S(2)}) collective-permute-start(bf16[3,128,256]{2,1,0:T(8,128)(2,1)S(1)} %get-tuple-element.72), channel_id=1, source_target_pairs={{0,16},{16,0},{32,48},{48,32},{64,80},{80,64},{96,112},{112,96},{1... | collective-permute-start | bytes 589832 | tf_op jit(solution)/shard_map/ppermute | solution.py:477
  71.6 9.1 %collective-permute-start.22 = (bf16[2,128,256]{2,1,0:T(8,128)(2,1)S(1)}, bf16[2,128,256]{2,1,0:T(8,128)(2,1)S(1)}, u32[]{:S(2)}, u32[]{:S(2)}) collective-permute-start(bf16[2,128,256]{2,1,0:T(8,128)(2,1)S(1)} %merge.1), channel_id=1, source_target_pairs={{32,0},{64,32},{96,64},{128,96},{160,128},{192,160},{224,192},{80,... | collective-permute-start | bytes 393224 | tf_op jit(solution)/shard_map/ppermute | solution.py:513
  80.7 7.3 %collective-permute-start.23 = (bf16[2,128,256]{2,1,0:T(8,128)(2,1)S(1)}, bf16[2,128,256]{2,1,0:T(8,128)(2,1)S(1)}, u32[]{:S(2)}, u32[]{:S(2)}) collective-permute-start(bf16[2,128,256]{2,1,0:T(8,128)(2,1)S(1)} %collective-permute-done.22.near_ref), channel_id=1, source_target_pairs={{0,16},{16,0},{32,48},{48,32},{64,80},{80,64},{96,112},{112,96},{1... | collective-permute-start | bytes 393224 | tf_op jit(solution)/shard_map/ppermute | solution.py:477
